TPU v7x, 128 devices: a whole 4x4x4 slice. The times are simulated.
128 devices in a mesh: ctx: 64 (over z, y, x), head: 2 (over core).
Axes of the slice: x: 4, y: 4, z: 4, core: 2. Of those that a mesh axis runs over, the one named last changes fastest.
Arguments:
- query: bfloat16 [24576, 6144], P(('ctx', 'head')), may hold values from -6 to 6
- key_in: bfloat16 [24576, 6144], P(('ctx', 'head')), may hold values from -6 to 6
- value: bfloat16 [24576, 6144], P(('ctx', 'head')), may hold values from -6 to 6
- cotangent: bfloat16 [24576, 6144], P(('ctx', 'head')), may hold values from -18 to 18
- decay_rate: float32 [48, 16], replicated, as said below
- residue: float32 [48, 16], replicated, may hold values from -2 to 2
Outputs:
- mixed: bfloat16 [24576, 6144], P(('ctx', 'head'))
- grad_query: bfloat16 [24576, 6144], P(('ctx', 'head'))
- grad_key: bfloat16 [24576, 6144], P(('ctx', 'head'))
- grad_value: bfloat16 [24576, 6144], P(('ctx', 'head'))
- residue_grad: float32 [48, 16], P('head')
Inputs may be any that keep to these rules, and one draw needn't show every extreme that they name: `decay_rate`: positive decay rates of at most 1/30.
All inputs are finite; a program needn't handle non-finite values.
Results may differ from a plain program's by a relative error of at most 0.00105.
Values may be sent and summed in bfloat16 or wider, within the bound.
No kernel may reach another device: no remote copies, remote signals or barrier semaphores. Data moves between devices by JAX's collectives and lax.ppermute only.
A program may use at most 192 MiB of HBM per device.

v0:
```python
import math

import jax
import jax.numpy as jnp
from jax import lax
from jax.sharding import PartitionSpec as P

HEAD_DIM = 128
SPAN = 768


HIGHEST = lax.Precision.HIGHEST


def entering_2(part, axis, combine, identity, reverse):
    count = lax.axis_size(axis)
    place = lax.axis_index(axis)
    ahead = count - 1 - place if reverse else place
    gathered = jax.tree.map(lambda a: lax.all_gather(a, axis), part)
    state = jax.tree.map(lambda a, e: jnp.zeros_like(a) + jnp.asarray(e, a.dtype), part, identity)

    def one(lap, state):
        source = count - 1 - lap if reverse else lap
        return combine(
            state, jax.tree.map(lambda a: lax.dynamic_index_in_dim(a, source, 0, False), gathered)
        )

    return lax.fori_loop(0, ahead, one, state)


def combine_states(earlier, later_part):
    return (earlier[0] * later_part[0], later_part[0][..., None] * earlier[1] + later_part[1])


def modal_layer(
    query,
    key_in,
    value,
    cotangent,
    decay_rate,
    residue,
    block_rows,
    forward_chain,
    backward_chain,
    seq_total,
):
    row_count, feature_count = query.shape
    head_count = decay_rate.shape[0]
    head_size = feature_count // head_count
    block_count = row_count // block_rows

    def blocked(source):
        return source.reshape(block_count, block_rows, head_count, head_size).astype(jnp.float32)

    query_wide = blocked(query)
    key_wide = blocked(key_in)
    value_wide = blocked(value)
    cotan_wide = blocked(cotangent)
    product = key_wide * value_wide
    norm_factor = jnp.sqrt(-jnp.expm1(-2.0 * decay_rate))
    coefficient = residue * norm_factor
    offsets = jnp.arange(block_rows, dtype=jnp.float32)
    decay_in = jnp.exp(-decay_rate[:, :, None] * offsets)
    decay_end = jnp.exp(-decay_rate[:, :, None] * (float(block_rows - 1) - offsets))
    growth = jnp.exp(decay_rate[:, :, None] * offsets)
    one_step = jnp.exp(-decay_rate)
    lag_index = lax.broadcasted_iota(jnp.int32, (block_rows, block_rows), 0) - lax.broadcasted_iota(
        jnp.int32, (block_rows, block_rows), 1
    )
    lower = lag_index[None] >= 0
    weighted_in = coefficient[:, :, None] * decay_in
    full_table = jnp.einsum("hmi,hmj->hij", weighted_in, growth, precision=HIGHEST)
    toeplitz = jnp.where(lower, full_table, 0.0)
    inner_part = jnp.einsum("hij,bjhc->bihc", toeplitz, product, precision=HIGHEST)
    block_ends = jnp.einsum("hmj,bjhc->bhmc", decay_end, product, precision=HIGHEST)
    block_decay = jnp.exp(-decay_rate * block_rows)[:, :, None]

    def walk_forward(state, block_end):
        return (block_decay * state + block_end, state)

    zero_state = jnp.zeros(block_ends.shape[1:], jnp.float32)
    device_total, entering_local = lax.scan(walk_forward, zero_state, block_ends)
    device_decay = jnp.exp(-decay_rate * row_count)
    incoming = forward_chain(device_decay, device_total)
    block_starts = jnp.arange(block_count, dtype=jnp.float32) * block_rows
    block_powers = jnp.exp(-decay_rate[None] * block_starts[:, None, None])[..., None]
    later_starts = (
        float(block_count - 1) - jnp.arange(block_count, dtype=jnp.float32)
    ) * block_rows
    later_powers = jnp.exp(-decay_rate[None] * later_starts[:, None, None])[..., None]
    entering = entering_local + block_powers * incoming[None]
    inflow = coefficient[:, :, None] * one_step[:, :, None] * decay_in
    outer_part = jnp.einsum("hmi,bhmc->bihc", inflow, entering, precision=HIGHEST)
    convolved = inner_part + outer_part
    mixed = (query_wide * convolved).reshape(row_count, feature_count).astype(jnp.bfloat16)
    grad_conv = cotan_wide * query_wide
    grad_query = (cotan_wide * convolved).reshape(row_count, feature_count).astype(jnp.bfloat16)
    back_inner = jnp.einsum("hij,bihc->bjhc", toeplitz, grad_conv, precision=HIGHEST)
    block_heads = jnp.einsum("hmi,bihc->bhmc", decay_in, grad_conv, precision=HIGHEST)

    def walk_backward(state, block_head):
        return (block_decay * state + block_head, state)

    back_total, later_local = lax.scan(walk_backward, zero_state, block_heads, reverse=True)
    outgoing = backward_chain(device_decay, back_total)
    later_states = later_local + later_powers * outgoing[None]
    outflow = coefficient[:, :, None] * one_step[:, :, None] * decay_end
    back_outer = jnp.einsum("hmj,bhmc->bjhc", outflow, later_states, precision=HIGHEST)
    grad_product = back_inner + back_outer
    grad_key = (grad_product * value_wide).reshape(row_count, feature_count).astype(jnp.bfloat16)
    grad_value = (grad_product * key_wide).reshape(row_count, feature_count).astype(jnp.bfloat16)
    cross_table = jnp.einsum("bihc,bjhc->hij", grad_conv, product, precision=HIGHEST)
    cross_lower = jnp.where(lower, cross_table, 0.0)
    grown_rows = jnp.einsum("hij,hmj->hmi", cross_lower, growth, precision=HIGHEST)
    near_terms = jnp.sum(grown_rows * decay_in, axis=2)
    far_terms = one_step * jnp.einsum("bhmc,bhmc->hm", block_heads, entering, precision=HIGHEST)
    residue_terms = norm_factor * (near_terms + far_terms) / math.sqrt(float(seq_total * HEAD_DIM))
    return (mixed, grad_query, grad_key, grad_value, residue_terms)


def on_device(query, key_in, value, cotangent, decay_rate, residue):
    seq_total = query.shape[0] * lax.axis_size("ctx") * lax.axis_size("head")
    group_heads = decay_rate.shape[0] // lax.axis_size("head")
    first_head = lax.axis_index("head") * group_heads
    local_rates = lax.dynamic_slice_in_dim(decay_rate, first_head, group_heads, 0)
    local_residue = lax.dynamic_slice_in_dim(residue, first_head, group_heads, 0)
    arrived = (
        lax.all_to_all(query, "head", split_axis=1, concat_axis=0, tiled=True),
        lax.all_to_all(key_in, "head", split_axis=1, concat_axis=0, tiled=True),
        lax.all_to_all(value, "head", split_axis=1, concat_axis=0, tiled=True),
        lax.all_to_all(cotangent, "head", split_axis=1, concat_axis=0, tiled=True),
    )
    block_rows = min(SPAN, arrived[0].shape[0])

    def forward_chain(decays, totals):
        return entering_2(
            (decays, totals),
            "ctx",
            combine_states,
            (jnp.ones_like(decays), jnp.zeros_like(totals)),
            False,
        )[1]

    def backward_chain(decays, totals):
        return entering_2(
            (decays, totals),
            "ctx",
            combine_states,
            (jnp.ones_like(decays), jnp.zeros_like(totals)),
            True,
        )[1]

    results = modal_layer(
        arrived[0],
        arrived[1],
        arrived[2],
        arrived[3],
        local_rates,
        local_residue,
        block_rows,
        forward_chain,
        backward_chain,
        seq_total,
    )
    returned = (
        lax.all_to_all(results[0], "head", split_axis=0, concat_axis=1, tiled=True),
        lax.all_to_all(results[1], "head", split_axis=0, concat_axis=1, tiled=True),
        lax.all_to_all(results[2], "head", split_axis=0, concat_axis=1, tiled=True),
        lax.all_to_all(results[3], "head", split_axis=0, concat_axis=1, tiled=True),
    )
    residue_grad = lax.psum(results[4], "ctx")
    return (returned[0], returned[1], returned[2], returned[3], residue_grad)


def solution(mesh):
    placed = (
        P(("ctx", "head"), None),
        P(("ctx", "head"), None),
        P(("ctx", "head"), None),
        P(("ctx", "head"), None),
        P(),
        P(),
    )
    return jax.shard_map(
        on_device,
        mesh=mesh,
        in_specs=placed,
        out_specs=(
            P(("ctx", "head"), None),
            P(("ctx", "head"), None),
            P(("ctx", "head"), None),
            P(("ctx", "head"), None),
            P("head", None),
        ),
        check_vma=False,
    )
```

profile of v0, /device:TPU:1, one launch (start us, length us, event | category | flops | bytes accessed | tf_op | source)
XLA Modules:
  0.0 1031.1 jit_solution(16150171669965274029)
XLA Ops:
  10.4 5.2 all-to-all-start.2
  19.1 6.6 all_to_all.116
  30.1 4.2 fusion.37
  37.6 5.3 all-to-all-start.4
  46.1 6.6 all_to_all.117
  59.2 155.4 %all-gather.1 = f32[64,24,16]{1,2,0:T(8,128)S(1)} all-gather(f32[1,24,16]{1,2,0:T(8,128)S(1)} %copy.92), channel_id=2, replica_groups=mesh['ctx'=64,'head'=2] {'ctx'}, dimensions={0}, use_global_device_ids=true | all-gather | bytes 99840 | tf_op jit(solution)/shard_map/all_gather | solution.py:19
  216.1 5.9 fusion.56
  228.2 6.1 copy.99
  239.7 6.1 copy.95
  251.2 6.0 copy.108
  260.9 6.1 copy.105
  267.0 15.8 %fusion.17 = f32[24,384,384]{2,1,0:T(8,128)S(1)} fusion(f32[384,24,128]{2,1,0:T(8,128)} %bitcast.123, f32[384,24,128]{2,1,0:T(8,128)} %bitcast.118), kind=kOutput, calls=%fused_computation.25 | convolution fusion | flops 5435817984 | bytes 23592960 | tf_op jit(solution)/shard_map/bihc,bjhc->hij/dot_general | solution.py:112
  282.9 13.5 %fusion.28 = f32[24,16]{1,0:T(8,128)S(1)} fusion(f32[24,384,384]{2,1,0:T(8,128)S(1)} %fusion.17, pred[384,384]{1,0:T(8,128)(4,1)S(1)} %subtract_compare_fusion, f32[24,16]{1,0:T(8,128)S(1)} %copy.119, f32[24,16]{1,0:T(8,128)S(1)} %get-tuple-element.240), kind=kOutput, calls=%fused_computation.42 | convolution fusion | flops 683605632 | bytes 14307840 | tf_op jit(solution)/shard_map/hij,hmj->hmi/dot_general | solution.py:114
  296.4 14.3 %fusion.42 = f32[24,384,384]{2,1,0:T(8,128)} fusion(f32[24,16]{1,0:T(8,128)S(1)} %copy.119, f32[24,16]{1,0:T(8,128)S(1)} %get-tuple-element.240, f32[24,16]{1,0:T(8,128)S(1)} %get-tuple-element.231), kind=kOutput, calls=%fused_computation.50 | convolution fusion | flops 679919616 | bytes 14160384 | tf_op jit(solution)/shard_map/hmi,hmj->hij/dot_general | solution.py:72
  310.7 23.5 %fusion.4 = f32[24,128,384]{2,1,0:T(8,128)} fusion(f32[24,384,384]{2,1,0:T(8,128)} %fusion.42, pred[384,384]{1,0:T(8,128)(4,1)S(1)} %subtract_compare_fusion, f32[384,24,128]{2,1,0:T(8,128)S(1)} %bitcast.121), kind=kOutput, calls=%fused_computation.8 | convolution fusion | flops 5439356928 | bytes 23740416 | tf_op jit(solution)/shard_map/hij,bjhc->bihc/dot_general | solution.py:74
  334.2 9.6 fusion.15
  349.4 34.3 %all_to_all.118 = bf16[2,192,3072]{2,1,0:T(8,128)(2,1)S(1)} all-to-all(bf16[2,192,3072]{2,1,0:T(8,128)(2,1)} %convert_element_type.134), channel_id=1, replica_groups=mesh['ctx'=64,'head'=2] {'head'}, dimensions={0} | all-to-all | bytes 4718592 | tf_op jit(solution)/shard_map/all_to_all | solution.py:166
  390.8 6.9 all_to_all.119
  399.3 398.9 %psum.7 = f32[24,16]{1,0:T(8,128)S(1)} all-reduce(f32[24,16]{1,0:T(8,128)S(1)} %get-tuple-element.236), channel_id=1, replica_groups=mesh['ctx'=64,'head'=2] {'ctx'}, use_global_device_ids=true, to_apply=%region_5.6 | all-reduce | flops 384 | bytes 3072 | tf_op jit(solution)/shard_map/psum | solution.py:171
  798.9 19.5 %fusion.2 = f32[24,128,384]{2,1,0:T(8,128)} fusion(f32[24,384,384]{2,1,0:T(8,128)} %fusion.42, pred[384,384]{1,0:T(8,128)(4,1)S(1)} %subtract_compare_fusion, f32[384,24,128]{2,1,0:T(8,128)} %bitcast.124), kind=kOutput, calls=%fused_computation.6 | convolution fusion | flops 5439356928 | bytes 23740416 | tf_op jit(solution)/shard_map/hij,bihc->bjhc/dot_general | solution.py:98
  818.4 112.8 %while.17 = (s32[]{:T(128)}, f32[24,16,128]{2,1,0:T(8,128)S(1)}, s32[]{:T(128)}, f32[64,24,16]{2,1,0:T(8,128)}, f32[64,24,16,128]{3,2,1,0:T(8,128)}, /*index=5*/s32[]{:T(128)}, s32[]{:T(128)}, s32[]{:T(128)}, s32[]{:T(128)}) while((s32[]{:T(128)}, f32[24,16,128]{2,1,0:T(8,128)S(1)}, s32[]{:T(128)}, f32[64,24,16]{2,1,0:T(8,128)}, ...), condition=%wide.region_3.4_spmd, body=%wide.region_2.3_spmd.sunk | while | flops 98310 | bytes 594587 | solution.py:28
  931.2 9.6 fusion.13
  946.4 62.1 %all_to_all.120 = bf16[2,192,3072]{2,1,0:T(8,128)(2,1)S(1)} all-to-all(bf16[2,192,3072]{2,1,0:T(8,128)(2,1)} %convert_element_type.146), channel_id=1, replica_groups=mesh['ctx'=64,'head'=2] {'head'}, dimensions={0} | all-to-all | bytes 4718592 | tf_op jit(solution)/shard_map/all_to_all | solution.py:168
  1015.6 6.8 all_to_all.121
  (191 shorter events, 186.6 us)
Async XLA Ops:
  7.2 8.5 copy-start.3
  7.2 8.5 copy-start.4
  10.4 8.6 all-to-all-start.2
  15.6 200.3 %all-gather.5.cloned.1.call-start = ((), (), s32[]{:S(2)}) async-start(), calls=%async_computation.8 | async-start | bytes 12779520 | tf_op jit(solution)/shard_map/all_gather | solution.py:19
  25.6 1.4 copy-start.1
  28.0 2.1 copy-start
  37.6 8.5 all-to-all-start.4
  42.8 775.6 %all-gather.7.cloned.1.call-start = ((), (), s32[]{:S(2)}) async-start(), calls=%async_computation.9 | async-start | bytes 12779520 | tf_op jit(solution)/shard_map/all_gather | solution.py:19
  52.7 3.4 copy-start.2
  282.9 27.9 %slice-start = ((s8[4718592]{0:T(1024)(128)(4,1)}), s8[4194304]{0:T(1024)(128)(4,1)S(1)}, s32[]{:S(2)}) async-start(s8[4718592]{0:T(1024)(128)(4,1)} %bitcast.119), calls=%async_computation.10 | async-start | bytes 8388608
  296.4 14.4 %slice-start.1 = ((s8[4718592]{0:T(1024)(128)(4,1)}), s8[524288]{0:T(1024)(128)(4,1)S(1)}, s32[]{:S(2)}) async-start(s8[4718592]{0:T(1024)(128)(4,1)} %bitcast.119), calls=%async_computation.11 | async-start | bytes 1048576
Sparse Core Ops, SparseCore 0:
  34.5 94.2 all-gather.4
  222.9 224.1 all-gather.6
where the time goes:
time: 1050 us; the launch traced here: 1030 us
  blocking collectives  678 us (65%)
  local copies, waits for them, and re-layouts  132 us (13%)
  matrix products  116 us (11%)
  other arithmetic  78.4 us (7%)
  between operations  14.5 us (1%)
    psum x1, blocking collectives, on_device(): residue_grad = lax.psum(results[4], 'ctx')  399 us
    all_gather x1, blocking collectives, entering_2(): gathered = jax.tree.map(lambda a: lax.all_gather(a, axis), part)  155 us
    add x63, other arithmetic, combine_states(): later_part[0][..., None] * earlier[1] + later_part[1]  66.1 us
    all_to_all x1, blocking collectives, on_device(): lax.all_to_all(results[2], 'head', split_axis=0, concat_axis=1, tiled=True)  62.1 us
    mul x63, local copies, waits for them, and re-layouts, combine_states(): later_part[0][..., None] * earlier[1] + later_part[1]  44.9 us
    all_to_all x1, blocking collectives, on_device(): lax.all_to_all(results[0], 'head', split_axis=0, concat_axis=1, tiled=True)  34.3 us
    convert_element_type x4, local copies, waits for them, and re-layouts, blocked(): source.reshape(block_count, block_rows, head_count, head_size)  24.3 us
    dot_general x1, matrix products, modal_layer(): jnp.einsum('hij,bjhc->bihc', toeplitz, product, precision=HIGHEST)  23.5 us
  transfers between devices with their start and end apart: 4, of which 0 were waited for; matrix products, arithmetic and copies ran while one was open for 17% of the time, Pallas kernels for 0%

commit v1 on v0

v1 whole, which is shorter than its diff:
```python
import math

import jax
import jax.numpy as jnp
from jax import lax
from jax.experimental import pallas as pl
from jax.experimental.pallas import tpu as pltpu
from jax.sharding import PartitionSpec as P

HEADS = 48
POLES = 16
WIDTH = 128
GROUP = 3
GROUPS = HEADS // GROUP
OWNERS = 8
ROWS = 64
F32 = jnp.float32
BF16 = jnp.bfloat16


def split(x):
    high = x.astype(BF16)
    return high, (x - high.astype(F32)).astype(BF16)


def mm(a, b):
    return jnp.dot(a, b, preferred_element_type=F32)


def mm_nt(a, b):
    return lax.dot_general(a, b, (((1,), (1,)), ((), ())), preferred_element_type=F32)


def head_of_row(shape, dim):
    return (lax.broadcasted_iota(jnp.int32, shape, dim) % 8) // 2


def states_kernel(rate_col, q_ref, k_ref, v_ref, c_ref, out_ref):
    rows = q_ref.shape[0]
    rate = rate_col[...][:, :1]
    step = lax.broadcasted_iota(jnp.int32, (ROWS, rows), 1).astype(F32)
    into = jnp.exp(-rate * step)
    ends = jnp.exp(-rate * (float(rows - 1) - step))
    into_hi, into_lo = split(into)
    ends_hi, ends_lo = split(ends)
    into_st = jnp.concatenate([into_hi, into_lo], 0)
    ends_st = jnp.concatenate([ends_hi, ends_lo], 0)
    owner_head = head_of_row((2 * ROWS, rows), 0)
    causal = lax.broadcasted_iota(jnp.int32, (rows, rows), 0) >= lax.broadcasted_iota(
        jnp.int32, (rows, rows), 1
    )
    fwd = jnp.zeros((ROWS, WIDTH), F32)
    bwd = jnp.zeros((ROWS, WIDTH), F32)
    near = jnp.zeros((ROWS, rows), F32)
    for h in range(GROUP):
        lanes = pl.ds(h * WIDTH, WIDTH)
        p_hi, p_lo = split(k_ref[:, lanes].astype(F32) * v_ref[:, lanes].astype(F32))
        g_hi, g_lo = split(c_ref[:, lanes].astype(F32) * q_ref[:, lanes].astype(F32))
        mine = owner_head == h
        zero = jnp.zeros((), BF16)
        in_h = jnp.where(mine, into_st, zero)
        en_h = jnp.where(mine, ends_st, zero)
        both = mm(en_h, p_hi)
        fwd += both[:ROWS] + both[ROWS:] + mm(en_h[:ROWS], p_lo)
        both = mm(in_h, g_hi)
        bwd += both[:ROWS] + both[ROWS:] + mm(in_h[:ROWS], g_lo)
        cross = mm_nt(g_hi, p_hi) + mm_nt(g_hi, p_lo) + mm_nt(g_lo, p_hi)
        x_hi, x_lo = split(jnp.where(causal, cross, 0.0))
        both = mm(in_h, x_hi)
        near += both[:ROWS] + both[ROWS:] + mm(in_h[:ROWS], x_lo)
    near_col = jnp.exp(rate * float(rows - 1)) * jnp.sum(near * ends, axis=1, keepdims=True)
    sub = lax.broadcasted_iota(jnp.int32, (ROWS, WIDTH), 0) % 8
    lane = lax.broadcasted_iota(jnp.int32, (ROWS, WIDTH), 1)
    near_rows = jnp.where(lane == sub, near_col, 0.0).reshape(OWNERS, 8, WIDTH).sum(axis=1)
    out_ref[:, :8, :] = fwd.reshape(OWNERS, 8, WIDTH)
    pad = jnp.broadcast_to(near_rows[:, None, :], (OWNERS, 8, WIDTH))
    row = lax.broadcasted_iota(jnp.int32, (OWNERS, 8, WIDTH), 1)
    out_ref[:, 8:, :] = jnp.where(row == 6, pad, bwd.reshape(OWNERS, 8, WIDTH))


def scan_kernel(place_ref, rate_ref, x_ref, out_ref, *, blocks, block_rows, scale):
    rate = rate_ref[...]
    sub = lax.broadcasted_iota(jnp.int32, (8, WIDTH), 0)
    lane = lax.broadcasted_iota(jnp.int32, (8, WIDTH), 1)
    over = jnp.exp(-rate * float(block_rows))
    zero = jnp.zeros((8, WIDTH), F32)

    def forward(e, carry):
        state, far, seen = carry
        adjoint = x_ref[e, 8:, :]
        out_ref[e, :8, :] = state
        return over * state + x_ref[e, :8, :], far + adjoint * state, seen + adjoint

    _, far, seen = lax.fori_loop(0, blocks, forward, (zero, zero, zero), unroll=8)
    near = jnp.where(lane == sub, jnp.broadcast_to(seen[6:7, :], (8, WIDTH)), 0.0)
    terms = jnp.where(sub < 6, jnp.exp(-rate) * far + near, 0.0)
    total = jnp.sum(terms, axis=1, keepdims=True)
    first = 2 * lax.rem(place_ref[0], OWNERS)

    def spread(h):
        hit = (sub == 2 * h + lane - first) & (lane >= first) & (lane < first + 2)
        return jnp.sum(jnp.where(hit, total * scale, 0.0), axis=0, keepdims=True)

    res0, res1, res2 = spread(0), spread(1), spread(2)
    pads = jnp.where(sub == 6, res0, res1)

    def backward(lap, state):
        e = blocks - 1 - lap
        out_ref[e, 6:8, :] = pads[6:8]
        out_ref[e, 8:, :] = jnp.where(sub == 6, res2, state)
        return over * state + x_ref[e, 8:, :]

    lax.fori_loop(0, blocks, backward, zero, unroll=8)


def toeplitz_kernel(rate_col, coef_col, rate_row, coef_row, q_ref, k_ref, v_ref, c_ref, conv_ref, grad_ref):
    rows = q_ref.shape[0]
    last = float(rows - 1)
    rate = rate_row[...].reshape(1, 3 * ROWS)
    coef = coef_row[...].reshape(1, 3 * ROWS)
    step = lax.broadcasted_iota(jnp.int32, (rows, 3 * ROWS), 0).astype(F32)
    third = lax.broadcasted_iota(jnp.int32, (rows, 3 * ROWS), 1) // ROWS
    owner_head = head_of_row((rows, 3 * ROWS), 1)

    def lefts(x):
        high, low = split(x)
        return jnp.where(third == 2, low, high)

    t_left = lefts(coef * jnp.exp(rate * (last - step)))
    u_left = lefts(jnp.exp(rate * step))
    rate_c = rate_col[...][:, :1]
    coef_c = coef_col[...][:, :1]
    across = lax.broadcasted_iota(jnp.int32, (ROWS, rows), 1).astype(F32)

    def rights(x):
        high, low = split(x)
        return jnp.concatenate([high, low, high], 0)

    t_right = rights(jnp.exp(-rate_c * (last - across)))
    u_right = rights(coef_c * jnp.exp(-rate_c * across))
    down = lax.broadcasted_iota(jnp.int32, (rows, rows), 0)
    right = lax.broadcasted_iota(jnp.int32, (rows, rows), 1)
    zero = jnp.zeros((), BF16)
    for h in range(GROUP):
        lanes = pl.ds(h * WIDTH, WIDTH)
        p_hi, p_lo = split(k_ref[:, lanes].astype(F32) * v_ref[:, lanes].astype(F32))
        g_hi, g_lo = split(c_ref[:, lanes].astype(F32) * q_ref[:, lanes].astype(F32))
        mine = owner_head == h
        t_hi, t_lo = split(jnp.where(down >= right, mm(jnp.where(mine, t_left, zero), t_right), 0.0))
        conv_ref[:, lanes] = mm(t_hi, p_hi) + mm(t_hi, p_lo) + mm(t_lo, p_hi)
        u_hi, u_lo = split(jnp.where(down <= right, mm(jnp.where(mine, u_left, zero), u_right), 0.0))
        grad_ref[:, lanes] = mm(u_hi, g_hi) + mm(u_hi, g_lo) + mm(u_lo, g_hi)


def output_kernel(
    rate_row, coef_row, s_ref, q_ref, k_ref, v_ref, c_ref, conv_ref, grad_ref,
    mixed_ref, gq_ref, gk_ref, gv_ref, res_ref,
):
    rows = q_ref.shape[0]
    rate = rate_row[...].reshape(1, 3 * ROWS)
    coef = coef_row[...].reshape(1, 3 * ROWS)
    step = lax.broadcasted_iota(jnp.int32, (rows, 3 * ROWS), 0).astype(F32)
    third = lax.broadcasted_iota(jnp.int32, (rows, 3 * ROWS), 1) // ROWS
    owner_head = head_of_row((rows, 3 * ROWS), 1)

    def lefts(x):
        high, low = split(x)
        return jnp.where(third == 2, low, high)

    inflow = lefts(coef * jnp.exp(-rate * (step + 1.0)))
    outflow = lefts(coef * jnp.exp(-rate * (float(rows) - step)))
    tile = s_ref[...]
    state = tile[:, :8, :].reshape(ROWS, WIDTH)
    later = tile[:, 8:, :].reshape(ROWS, WIDTH)

    def rights(x):
        high, low = split(x)
        return jnp.concatenate([high, low, high], 0)

    state_st = rights(state)
    later_st = rights(later)
    zero = jnp.zeros((), BF16)
    for h in range(GROUP):
        lanes = pl.ds(h * WIDTH, WIDTH)
        mine = owner_head == h
        conv = conv_ref[:, lanes] + mm(jnp.where(mine, inflow, zero), state_st)
        mixed_ref[:, lanes] = (q_ref[:, lanes].astype(F32) * conv).astype(BF16)
        gq_ref[:, lanes] = (c_ref[:, lanes].astype(F32) * conv).astype(BF16)
        grad = grad_ref[:, lanes] + mm(jnp.where(mine, outflow, zero), later_st)
        gk_ref[:, lanes] = (grad * v_ref[:, lanes].astype(F32)).astype(BF16)
        gv_ref[:, lanes] = (grad * k_ref[:, lanes].astype(F32)).astype(BF16)
    sub = lax.broadcasted_iota(jnp.int32, (8, WIDTH), 0)
    res = jnp.zeros((8, WIDTH), F32)
    for h in range(GROUP):
        spot = (6, 7, 14)[h]
        line = jnp.sum(tile[:, spot, :], axis=0, keepdims=True)
        res = jnp.where(sub == h, line, res)
    res_ref[0] = res


def by_owner(table):
    rows = table.reshape(GROUPS, GROUP, OWNERS, 2).transpose(0, 2, 1, 3)
    return jnp.pad(rows.reshape(GROUPS * OWNERS, 2 * GROUP), ((0, 0), (0, 2)))


def on_device(query, key_in, value, cotangent, decay_rate, residue):
    blocks = lax.axis_size("ctx") * lax.axis_size("head")
    place = lax.axis_index("ctx") * lax.axis_size("head") + lax.axis_index("head")
    rows, width = query.shape
    norm = jnp.sqrt(-jnp.expm1(-2.0 * decay_rate))
    rates = by_owner(decay_rate)
    coefs = by_owner(residue * norm)
    norms = by_owner(norm)
    rate_col = jnp.broadcast_to(rates.reshape(-1, 1), (GROUPS * ROWS, WIDTH))
    coef_col = jnp.broadcast_to(coefs.reshape(-1, 1), (GROUPS * ROWS, WIDTH))
    rate_row = jnp.tile(rates.reshape(GROUPS, 1, ROWS), (1, 1, 3))
    coef_row = jnp.tile(coefs.reshape(GROUPS, 1, ROWS), (1, 1, 3))
    own_rate = jnp.broadcast_to(lax.dynamic_index_in_dim(rates, place, 0, False)[:, None], (8, WIDTH))
    own_norm = jnp.broadcast_to(lax.dynamic_index_in_dim(norms, place, 0, False)[:, None], (8, WIDTH))

    wide = pl.BlockSpec((rows, GROUP * WIDTH), lambda g: (0, g))
    col = pl.BlockSpec((ROWS, WIDTH), lambda g: (g, 0))
    row = pl.BlockSpec((1, 1, 3 * ROWS), lambda g: (g, 0, 0))
    tile = pl.BlockSpec((OWNERS, 16, WIDTH), lambda g: (g, 0, 0))
    wide_bytes = 2 * rows * width
    states = pl.pallas_call(
        states_kernel,
        grid=(GROUPS,),
        in_specs=[col, wide, wide, wide, wide],
        out_specs=tile,
        out_shape=jax.ShapeDtypeStruct((GROUPS * OWNERS, 16, WIDTH), F32),
        cost_estimate=pl.CostEstimate(flops=10**10, bytes_accessed=5 * wide_bytes, transcendentals=0),
        name="states",
    )(rate_col, query, key_in, value, cotangent)
    gathered = lax.all_to_all(states, ("ctx", "head"), split_axis=0, concat_axis=0, tiled=True)

    conv, grad = pl.pallas_call(
        toeplitz_kernel,
        grid=(GROUPS,),
        in_specs=[col, col, row, row, wide, wide, wide, wide],
        out_specs=[wide, wide],
        out_shape=[jax.ShapeDtypeStruct((rows, width), F32)] * 2,
        cost_estimate=pl.CostEstimate(flops=10**10, bytes_accessed=8 * wide_bytes, transcendentals=0),
        name="toeplitz",
    )(rate_col, coef_col, rate_row, coef_row, query, key_in, value, cotangent)

    whole = pl.BlockSpec(memory_space=pltpu.VMEM)
    scanned = pl.pallas_call(
        lambda place_ref, rate_ref, norm_ref, x_ref, out_ref: scan_kernel(
            place_ref,
            rate_ref,
            x_ref,
            out_ref,
            blocks=blocks,
            block_rows=rows,
            scale=norm_ref[...][:, :1] / math.sqrt(float(rows * blocks * WIDTH)),
        ),
        in_specs=[pl.BlockSpec(memory_space=pltpu.SMEM), whole, whole, whole],
        out_specs=whole,
        out_shape=jax.ShapeDtypeStruct((blocks, 16, WIDTH), F32),
        cost_estimate=pl.CostEstimate(flops=10**6, bytes_accessed=2**21, transcendentals=0),
        name="scan",
    )(place.reshape(1), own_rate, own_norm, gathered)
    entering = lax.all_to_all(scanned, ("ctx", "head"), split_axis=0, concat_axis=0, tiled=True)

    out = jax.ShapeDtypeStruct((rows, width), BF16)
    mixed, grad_query, grad_key, grad_value, res = pl.pallas_call(
        output_kernel,
        grid=(GROUPS,),
        in_specs=[row, row, tile, wide, wide, wide, wide, wide, wide],
        out_specs=[wide, wide, wide, wide, pl.BlockSpec((1, 8, WIDTH), lambda g: (g, 0, 0))],
        out_shape=[out, out, out, out, jax.ShapeDtypeStruct((GROUPS, 8, WIDTH), F32)],
        cost_estimate=pl.CostEstimate(flops=10**9, bytes_accessed=12 * wide_bytes, transcendentals=0),
        name="outputs",
    )(rate_row, coef_row, entering, query, key_in, value, cotangent, conv, grad)
    half = GROUPS // lax.axis_size("head")
    mine = lax.dynamic_slice_in_dim(res, lax.axis_index("head") * half, half, 0)
    residue_grad = mine[:, :GROUP, :POLES].reshape(half * GROUP, POLES)
    return mixed, grad_query, grad_key, grad_value, residue_grad


def solution(mesh):
    wide = P(("ctx", "head"), None)
    return jax.shard_map(
        on_device,
        mesh=mesh,
        in_specs=(wide, wide, wide, wide, P(), P()),
        out_specs=(wide, wide, wide, wide, P("head", None)),
        check_vma=False,
    )
```

time: 1050 us -> 113 us (0.11); the launches traced: 1030 us -> 112 us
  blocking collectives: 678 us -> 0 us
  local copies, waits for them, and re-layouts: 132 us -> 10.2 us
  matrix products: 116 us -> 0 us
  other arithmetic: 78.4 us -> 0.02 us
  Pallas kernels: 0 us -> 66.4 us
  waiting for transfers between devices: 0.04 us -> 18.5 us
  between operations: 14.5 us -> 0.76 us
    psum x1 -> x0, blocking collectives: 399 us -> none  [on_device(): residue_grad = lax.psum(results[4], 'ctx')]
    all_gather x1 -> x0, blocking collectives: 155 us -> none  [entering_2(): gathered = jax.tree.map(lambda a: lax.all_gather(a, axis), part)]
    all_to_all x6 -> x0, blocking collectives: 123 us -> none  [the longest x1 62.1 us: on_device(): lax.all_to_all(results[2], 'head', split_axis=0, concat_axis=1, tiled=True)]
    dot_general x9 -> x0, matrix products: 116 us -> none  [the longest x1 23.5 us: modal_layer(): jnp.einsum('hij,bjhc->bihc', toeplitz, product, precision=HIGHEST)]
    add x64 -> x0, other arithmetic: 66.9 us -> none  [the longest x63 66.1 us: combine_states(): later_part[0][..., None] * earlier[1] + later_part[1]]
    pallas_call x0 -> x4, Pallas kernels: none -> 66.4 us  [the longest x1 23.3 us: on_device(): pl.pallas_call(states_kernel, grid=(GROUPS,), in_specs=[col, wide, wide,...]
    convert_element_type x12 -> x0, local copies, waits for them, and re-layouts: 46.4 us -> none  [the longest x4 24.3 us: blocked(): source.reshape(block_count, block_rows, head_count, head_size)]
    mul x63 -> x0, local copies, waits for them, and re-layouts: 44.9 us -> none  [combine_states(): later_part[0][..., None] * earlier[1] + later_part[1]]
  transfers between devices with their start and end apart: 4 -> 2, of which waited for: 0 -> 1; matrix products, arithmetic and copies ran while one was open for 17% -> 4% of each run, Pallas kernels for 0% -> 20%
where the time goes in v1:
time: 113 us; the launch traced here: 112 us
  Pallas kernels  66.4 us (59%)
  waiting for transfers between devices  18.5 us (16%)
  starting transfers between devices  15.9 us (14%)
  local copies, waits for them, and re-layouts  10.2 us (9%)
    pallas_call x1, Pallas kernels, on_device(): pl.pallas_call(states_kernel, grid=(GROUPS,), in_specs=[col, wide, wide,...  23.3 us
    pallas_call x1, Pallas kernels, on_device(): pl.pallas_call(toeplitz_kernel, grid=(GROUPS,), in_specs=[col, col, row,...  22.1 us
    all_to_all x1, waiting for transfers between devices, on_device(): lax.all_to_all(states, ('ctx', 'head'), split_axis=0, concat_axis=0, tile...  18.5 us
    pallas_call x1, Pallas kernels, on_device(): pl.pallas_call(output_kernel, grid=(GROUPS,), in_specs=[row, row, tile, w...  18.1 us
    all_to_all x1, starting transfers between devices, on_device(): lax.all_to_all(states, ('ctx', 'head'), split_axis=0, concat_axis=0, tile...  11.5 us
    all_to_all x1, starting transfers between devices, on_device(): lax.all_to_all(scanned, ('ctx', 'head'), split_axis=0, concat_axis=0, til...  4.43 us
    pallas_call x1, Pallas kernels, on_device(): pl.pallas_call(lambda place_ref, rate_ref, norm_ref, x_ref, out_ref: scan...  2.95 us
  transfers between devices with their start and end apart: 2, of which 1 were waited for; matrix products, arithmetic and copies ran while one was open for 4% of the time, Pallas kernels for 20%

profile of v1, /device:TPU:1, one launch (start us, length us, event | category | flops | bytes accessed | tf_op | source)
XLA Modules:
  0.0 111.7 jit_solution(15388471626963979753)
XLA Ops:
  0.6 0.8 reshape.54
  1.4 0.3 copy.26
  1.8 0.1 copy.39
  2.0 1.0 broadcast_in_dim.35.rate_col
  3.0 23.3 %states.1 = f32[128,16,128]{2,1,0:T(8,128)} custom-call(f32[1024,128]{1,0:T(8,128)} %broadcast_in_dim.35.rate_col, bf16[192,6144]{1,0:T(8,128)(2,1)} %q_ref.5, bf16[192,6144]{1,0:T(8,128)(2,1)} %k_ref.5, bf16[192,6144]{1,0:T(8,128)(2,1)} %v_ref.5, bf16[192,6144]{1,0:T(8,128)(2,1)} %c_ref.5), custom_call_target="tpu_custom_call" | custom-call | flops 10000000000 | bytes 11796480 | tf_op jit(solution)/shard_map/states/pallas_call | solution.py:226
  26.3 11.5 %all-to-all-start = ((f32[128,16,128]{2,1,0:T(8,128)}), f32[128,16,128]{2,1,0:T(8,128)S(1)}, u32[]{:S(2)}, u32[]{:S(2)}) async-start(f32[128,16,128]{2,1,0:T(8,128)} %states.1), calls=%async_computation | async-start | bytes 2097152 | tf_op jit(solution)/shard_map/all_to_all | solution.py:235
  37.8 0.1 reshape.59
  37.9 0.3 copy.30
  38.3 0.2 dynamic-slice_reduce_fusion
  38.5 18.5 %all-to-all-done.x_ref = f32[128,16,128]{2,1,0:T(8,128)S(1)} async-done(((f32[128,16,128]{2,1,0:T(8,128)}), f32[128,16,128]{2,1,0:T(8,128)S(1)}, u32[]{:S(2)}, u32[]{:S(2)}) %all-to-all-start) | async-done | bytes 1048608 | tf_op jit(solution)/shard_map/all_to_all | solution.py:235
  57.0 0.8 broadcast_in_dim.33.norm_ref
  57.8 0.7 broadcast_in_dim.31.rate_ref
  58.4 3.0 %scan.1 = f32[128,16,128]{2,1,0:T(8,128)} custom-call(s32[1]{0:T(128)} %bitcast.2.place_ref, f32[8,128]{1,0:T(8,128)} %broadcast_in_dim.31.rate_ref, f32[8,128]{1,0:T(8,128)} %broadcast_in_dim.33.norm_ref, f32[128,16,128]{2,1,0:T(8,128)} %copy-done.1), custom_call_target="tpu_custom_call" | custom-call | flops 1000000 | bytes 2097152 | tf_op jit(solution)/shard_map/scan/pallas_call | solution.py:248
  61.4 4.4 %all-to-all-start.1 = ((f32[128,16,128]{2,1,0:T(8,128)}), f32[128,16,128]{2,1,0:T(8,128)S(1)}, u32[]{:S(2)}, u32[]{:S(2)}) async-start(f32[128,16,128]{2,1,0:T(8,128)} %scan.1), calls=%async_computation.1 | async-start | bytes 2097152 | tf_op jit(solution)/shard_map/all_to_all | solution.py:264
  65.9 0.3 copy.28
  66.3 0.1 copy.38
  66.7 0.7 tile.27.coef_row
  67.4 0.7 tile.26.rate_row
  68.1 1.0 broadcast_in_dim.37.coef_col
  69.1 22.1 %toeplitz.1 = (f32[192,6144]{1,0:T(8,128)}, f32[192,6144]{1,0:T(8,128)}) custom-call(f32[1024,128]{1,0:T(8,128)} %broadcast_in_dim.35.rate_col, f32[1024,128]{1,0:T(8,128)} %broadcast_in_dim.37.coef_col, f32[16,1,192]{2,1,0:T(1,128)} %tile.26.rate_row, f32[16,1,192]{2,1,0:T(1,128)} %tile.27.coef_row, bf16[192,6144]{1,0:T(8,128)(2,1)} %q_ref.5, ...), custom_call_target="tpu_custom_call" | custom-call | flops 10000000000 | bytes 18874368 | tf_op jit(solution)/shard_map/toeplitz/pallas_call | solution.py:237
  91.2 1.0 copy-done
  92.1 18.1 %outputs.1 = (bf16[192,6144]{1,0:T(8,128)(2,1)}, bf16[192,6144]{1,0:T(8,128)(2,1)}, bf16[192,6144]{1,0:T(8,128)(2,1)}, bf16[192,6144]{1,0:T(8,128)(2,1)}, f32[16,8,128]{2,1,0:T(8,128)}) custom-call(f32[16,1,192]{2,1,0:T(1,128)} %tile.26.rate_row, f32[16,1,192]{2,1,0:T(1,128)} %tile.27.coef_row, f32[128,16,128]{2,1,0:T(8,128)} %copy-done, ...), custom_call_target="tpu_custom_call" | custom-call | flops 1000000000 | bytes 28311552 | tf_op jit(solution)/shard_map/outputs/pallas_call | solution.py:267
  110.2 0.8 constant_dynamic-slice_fusion
  111.0 0.7 copy.37
  (22 shorter events, 0.8 us)
Async XLA Ops:
  3.0 34.8 %copy-start.2 = (f32[48,16]{0,1:T(8,128)S(1)}, f32[48,16]{0,1:T(8,128)}, u32[]{:S(2)}) copy-start(f32[48,16]{0,1:T(8,128)} %param.10) | copy-start | bytes 9220
  3.0 34.8 %copy-start.3 = (f32[48,16]{0,1:T(8,128)S(1)}, f32[48,16]{0,1:T(8,128)}, u32[]{:S(2)}) copy-start(f32[48,16]{0,1:T(8,128)} %param.11) | copy-start | bytes 9220
  26.3 30.7 %all-to-all-start = ((f32[128,16,128]{2,1,0:T(8,128)}), f32[128,16,128]{2,1,0:T(8,128)S(1)}, u32[]{:S(2)}, u32[]{:S(2)}) async-start(f32[128,16,128]{2,1,0:T(8,128)} %states.1), calls=%async_computation | async-start | bytes 2097152 | tf_op jit(solution)/shard_map/all_to_all | solution.py:235
  57.0 1.4 %copy-start.1 = (f32[128,16,128]{2,1,0:T(8,128)}, f32[128,16,128]{2,1,0:T(8,128)S(1)}, u32[]{:S(2)}) copy-start(f32[128,16,128]{2,1,0:T(8,128)S(1)} %all-to-all-done.x_ref) | copy-start | bytes 3145732
  61.4 29.8 %all-to-all-start.1 = ((f32[128,16,128]{2,1,0:T(8,128)}), f32[128,16,128]{2,1,0:T(8,128)S(1)}, u32[]{:S(2)}, u32[]{:S(2)}) async-start(f32[128,16,128]{2,1,0:T(8,128)} %scan.1), calls=%async_computation.1 | async-start | bytes 2097152 | tf_op jit(solution)/shard_map/all_to_all | solution.py:264
  91.1 1.0 copy-start

commit v2 on v0

v2 whole, which is shorter than its diff:
```python
import functools
import math

import jax
import jax.numpy as jnp
from jax import lax
from jax.experimental import pallas as pl
from jax.experimental.pallas import tpu as pltpu
from jax.sharding import PartitionSpec as P

HEADS = 48
POLES = 16
WIDTH = 128
GROUP = 3
GROUPS = HEADS // GROUP
PACK = 4
OWNERS = 8
UNITS = 2 * GROUP
CHUNK = 64
BATCH = {"states": 4, "near": 4, "local": 4, "outputs": 4}
F32 = jnp.float32
BF16 = jnp.bfloat16
VMEM_LIMIT = 12 * 2**20


def split(x):
    high = x.astype(BF16)
    return high, (x - high.astype(F32)).astype(BF16)


def iota(shape, dim):
    return lax.broadcasted_iota(jnp.int32, shape, dim)


def mm(a, b):
    return jnp.dot(a, b, preferred_element_type=F32)


def mm_nt(a, b):
    return lax.dot_general(a, b, (((1,), (1,)), ((), ())), preferred_element_type=F32)


def mm_tn(a, b):
    return lax.dot_general(a, b, (((0,), (0,)), ((), ())), preferred_element_type=F32)


def stacked(x, parts=(0, 1, 0)):
    both = split(x)
    return jnp.concatenate([both[p] for p in parts], 0)


def column(table, head, first=0, count=POLES):
    hit = iota((count, HEADS), 1) == head
    return jnp.sum(jnp.where(hit, table[first : first + count, :], 0.0), axis=1, keepdims=True)


def product(a_ref, b_ref, lanes):
    return split(a_ref[:, lanes].astype(F32) * b_ref[:, lanes].astype(F32))


def lanes_of(at, h):
    return pl.ds(pl.multiple_of((at * GROUP + h) * WIDTH, WIDTH), WIDTH)


def each_batch(batch, body):
    def lap(n, _):
        body([(n * batch + j, pl.program_id(0) * PACK + n * batch + j) for j in range(batch)])
        return 0

    lax.fori_loop(0, PACK // batch, lap, 0)


def sublane_of(owner, unit):
    return lax.rem(owner + 8 - unit, 8)


def read_unit(ref, at, u, first):
    sub = iota((8, WIDTH), 0)
    tile = jnp.zeros((8, WIDTH), F32)
    for owner in range(OWNERS):
        tile = jnp.where(sub == (owner - u) % 8, ref[at * OWNERS + owner, pl.ds(first, 8), :], tile)
    return tile


def read_head(ref, at, h, first):
    return jnp.concatenate([read_unit(ref, at, 2 * h, first), read_unit(ref, at, 2 * h + 1, first)], 0)


def states_kernel(rate_ref, q_ref, k_ref, v_ref, c_ref, out_ref):
    rows = q_ref.shape[0]
    spot = iota((POLES, rows), 1).astype(F32)
    sub = iota((8, WIDTH), 0)

    def batch(groups):
        for at, number in groups:
            ahead, back = [], []
            for h in range(GROUP):
                lanes = lanes_of(at, h)
                rate = column(rate_ref, number * GROUP + h)

                def state(weights, high, low):
                    w_hi, w_lo = split(weights)
                    both = mm(jnp.concatenate([w_hi, w_lo], 0), high)
                    return both[:POLES] + both[POLES:] + mm(w_hi, low)

                fwd = state(jnp.exp(-rate * (float(rows - 1) - spot)), *product(k_ref, v_ref, lanes))
                bwd = state(jnp.exp(-rate * spot), *product(c_ref, q_ref, lanes))
                ahead += [fwd[:8], fwd[8:]]
                back += [bwd[:8], bwd[8:]]
            for owner in range(OWNERS):
                for first, units in ((0, ahead), (8, back)):
                    tile = jnp.zeros((8, WIDTH), F32)
                    for u in range(UNITS):
                        tile = jnp.where(sub == (owner - u) % 8, units[u], tile)
                    out_ref[at * OWNERS + owner, first : first + 8, :] = tile

    each_batch(BATCH["states"], batch)


def near_kernel(
    rate_ref, norm_ref, q_ref, k_ref, v_ref, c_ref,
    out_ref, part_ref, ph_ref, pl_ref, gh_ref, gl_ref, *, scale,
):
    rows = q_ref.shape[0]
    chunks = rows // CHUNK
    step = pl.program_id(0)
    spot = iota((POLES, chunks * CHUNK), 1)
    local = (spot % CHUNK).astype(F32)
    causal = iota((CHUNK, CHUNK), 0) >= iota((CHUNK, CHUNK), 1)
    lane = iota((8, WIDTH), 1)
    sub = iota((8, WIDTH), 0)
    wide = iota((POLES, WIDTH), 1) % POLES == iota((POLES, WIDTH), 0)

    @pl.when(step == 0)
    def _():
        out_ref[...] = jnp.zeros_like(out_ref)

    def part_states(weights, high, low):
        w_hi, w_lo = split(weights)
        zero = jnp.zeros((), BF16)
        w_hi = jnp.concatenate([jnp.where(spot // CHUNK == c, w_hi, zero) for c in range(chunks)], 0)
        w_lo = jnp.concatenate([jnp.where(spot // CHUNK == c, w_lo, zero) for c in range(chunks)], 0)
        both = mm(jnp.concatenate([w_hi, w_lo], 0), high)
        return both[: chunks * POLES] + both[chunks * POLES :] + mm(w_hi, low)

    def batch(groups):
        heads = [(at * GROUP + h, number * GROUP + h, lanes_of(at, h)) for at, number in groups for h in range(GROUP)]
        crosses, moves, parts, total = [], [], [], out_ref[...]
        for at, head, lanes in heads:
            p_hi, p_lo = product(k_ref, v_ref, lanes)
            g_hi, g_lo = product(c_ref, q_ref, lanes)
            ph_ref[:, lanes], pl_ref[:, lanes] = p_hi, p_lo
            gh_ref[:, lanes], gl_ref[:, lanes] = g_hi, g_lo
            rate = column(rate_ref, head)
            f = part_states(jnp.exp(-rate * (float(CHUNK - 1) - local)), p_hi, p_lo)
            b = part_states(jnp.exp(-rate * local), g_hi, g_lo)
            part_ref[at, 0], part_ref[at, 1] = f, b
            parts.append((f, b))
            cross = jnp.zeros((2 * CHUNK, 2 * CHUNK), F32)
            for c in range(chunks):
                span = slice(c * CHUNK, (c + 1) * CHUNK)
                left = jnp.concatenate([g_hi[span], g_lo[span]], 0)
                right = jnp.concatenate([p_hi[span], p_lo[span]], 0)
                cross += mm_nt(left, right)
            cross = cross[:CHUNK, :CHUNK] + (cross[:CHUNK, CHUNK:] + cross[CHUNK:, :CHUNK])
            crosses.append(stacked(jnp.where(causal, cross, 0.0)))
        for cross, (_, head, _) in zip(crosses, heads):
            into_hi, into_lo = split(jnp.exp(-column(rate_ref, head) * local))
            moves.append(mm(jnp.where(spot // CHUNK == 2, into_lo, into_hi), cross))
        for moved, (f, b), (_, head, _) in zip(moves, parts, heads):
            rate = column(rate_ref, head)
            over = jnp.exp(-rate * float(CHUNK))
            ends = jnp.exp(-rate * (float(CHUNK - 1) - local[:, :CHUNK]))
            near = jnp.exp(rate * float(CHUNK - 1)) * jnp.sum(moved * ends, axis=1, keepdims=True)
            state = f[:POLES]
            far = jnp.zeros((POLES, WIDTH), F32)
            for c in range(1, chunks):
                far += b[c * POLES : (c + 1) * POLES] * state
                state = f[c * POLES : (c + 1) * POLES] + over * state
            near += jnp.exp(-rate) * jnp.sum(far, axis=1, keepdims=True)
            near *= column(norm_ref, head) * scale
            line = jnp.sum(jnp.where(wide, near, 0.0), axis=0, keepdims=True)
            total += jnp.where((sub == head // 8) & (lane // POLES == head % 8), line, 0.0)
        out_ref[...] = total

    each_batch(BATCH["near"], batch)


def local_kernel(rate_ref, coef_ref, part_ref, ph_ref, pl_ref, gh_ref, gl_ref, conv_ref, grad_ref):
    chunks = ph_ref.shape[0] // CHUNK
    wide = 3 * CHUNK + 3 * POLES
    lane_t = iota((POLES, wide), 1)
    hit = (lane_t - 3 * CHUNK) % POLES == iota((POLES, wide), 0)
    ramp = (lane_t % CHUNK).astype(F32)
    here = iota((POLES, CHUNK), 1).astype(F32)
    down = iota((CHUNK, wide), 0)
    lane = iota((CHUNK, wide), 1)
    low_part = ((lane >= 2 * CHUNK) & (lane < 3 * CHUNK)) | (lane >= 3 * CHUNK + 2 * POLES)

    def batch(groups):
        heads = [(at * GROUP + h, number * GROUP + h, lanes_of(at, h)) for at, number in groups for h in range(GROUP)]
        done = []
        for side, (high_ref, low_ref, out_ref) in enumerate(((ph_ref, pl_ref, conv_ref), (gh_ref, gl_ref, grad_ref))):
            flip = (lambda x: float(CHUNK - 1) - x) if side else (lambda x: x)
            keep = ((down <= lane % CHUNK) if side else (down >= lane % CHUNK)) | (lane >= 3 * CHUNK)
            tables = []
            for _, head, _ in heads:
                rate = column(rate_ref, head)
                left = column(coef_ref, head) * jnp.exp(-rate * flip(here))
                right = jnp.where(
                    lane_t < 3 * CHUNK, jnp.exp(rate * flip(ramp)), jnp.where(hit, jnp.exp(-rate), 0.0)
                )
                table = mm_tn(stacked(left, (0, 0, 1)), stacked(right))
                t_hi, t_lo = split(jnp.where(keep, table, 0.0))
                tables.append(jnp.where(low_part, t_lo, t_hi))
            for table, (at, head, lanes) in zip(tables, heads):
                over = jnp.exp(-column(rate_ref, head) * float(CHUNK))
                state = jnp.zeros((POLES, WIDTH), F32)
                for c in reversed(range(chunks)) if side else range(chunks):
                    span = slice(c * CHUNK, (c + 1) * CHUNK)
                    s_hi, s_lo = split(state)
                    high, low = high_ref[span, lanes], low_ref[span, lanes]
                    source = jnp.concatenate([high, low, high, s_hi, s_lo, s_hi], 0)
                    done.append((out_ref, span, lanes, mm(table, source)))
                    state = part_ref[at, side, c * POLES : (c + 1) * POLES] + over * state
        for out_ref, span, lanes, value in done:
            out_ref[span, lanes] = value

    each_batch(BATCH["local"], batch)


def scan_kernel(place_ref, rate_ref, norm_ref, near_ref, x_ref, out_ref, *, block_rows, scale):
    blocks = x_ref.shape[0]
    group = place_ref[0] // OWNERS
    owner = lax.rem(place_ref[0], OWNERS)
    sub = iota((8, WIDTH), 0)
    lane = iota((8, WIDTH), 1)
    zero = jnp.zeros((8, WIDTH), F32)

    def own(table):
        rows = zero
        for u in range(UNITS):
            rows = jnp.where(
                sub == sublane_of(owner, u), column(table, group * GROUP + u // 2, 8 * (u % 2), 8), rows
            )
        return rows

    rate = own(rate_ref)
    over = jnp.exp(-rate * float(block_rows))

    def forward(e, carry):
        state, far = carry
        out_ref[e, :8, :] = state
        return over * state + x_ref[e, :8, :], far + x_ref[e, 8:, :] * state

    _, far = lax.fori_loop(0, blocks, forward, (zero, zero), unroll=8)
    far = jnp.sum(far * jnp.exp(-rate), axis=1, keepdims=True) * own(norm_ref) * scale
    total = near_ref[...]
    for u in range(UNITS):
        at = sublane_of(owner, u)
        head = group * GROUP + u // 2
        value = jnp.sum(jnp.where(sub == at, far, 0.0), axis=0, keepdims=True)
        spot = POLES * lax.rem(head, 8) + 8 * (u % 2) + at
        total += jnp.where((sub == head // 8) & (lane == spot), value, 0.0)
    used = zero == 0.0
    pads = [[zero, zero], [zero, zero]]
    for u, side, line in ((6, 0, 0), (7, 0, 1), (6, 1, 2), (7, 1, None)):
        at = sub == sublane_of(owner, u)
        used = used & ~at
        if line is not None:
            for k in range(2):
                pads[k][side] = jnp.where(at, total[3 * k + line : 3 * k + line + 1], pads[k][side])

    def backward(lap, state):
        for k in (1, 0):
            e = blocks - 2 - 2 * lap + k
            out_ref[e, :8, :] = jnp.where(used, out_ref[e, :8, :], pads[k][0])
            out_ref[e, 8:, :] = jnp.where(used, state, pads[k][1])
            state = over * state + x_ref[e, 8:, :]
        return state

    lax.fori_loop(0, blocks // 2, backward, zero, unroll=4)


def output_kernel(
    rate_ref, coef_ref, s_ref, q_ref, k_ref, v_ref, c_ref, conv_ref, grad_ref,
    mixed_ref, gq_ref, gk_ref, gv_ref, res_ref, sums,
):
    rows = q_ref.shape[0]
    spot = iota((POLES, rows), 1).astype(F32)
    sub = iota((8, WIDTH), 0)
    step = pl.program_id(0)

    @pl.when(step == 0)
    def _():
        sums[...] = jnp.zeros_like(sums)

    res = sums[...]
    for at in range(PACK):
        for u, first, line in ((6, 0, 0), (7, 0, 1), (6, 8, 2)):
            value = jnp.zeros((1, WIDTH), F32)
            for owner in range(OWNERS):
                row = first + (owner - u) % 8
                value += s_ref[at * OWNERS + owner, row : row + 1, :]
            res += jnp.where(sub == line, value, 0.0)
    sums[...] = res

    @pl.when(step == pl.num_programs(0) - 1)
    def _():
        half = HEADS // 2
        wide = iota((POLES, WIDTH), 1) % POLES == iota((POLES, WIDTH), 0)
        source = iota((WIDTH, half), 0) // POLES
        target = iota((WIDTH, half), 1)
        out = jnp.zeros((POLES, half), F32)
        for line in range(half * POLES // WIDTH):
            high, low = split(jnp.where(wide, sums[line : line + 1, :], 0.0))
            pick = jnp.where(target == 8 * line + source, 1.0, 0.0).astype(BF16)
            out += mm(high, pick) + mm(low, pick)
        res_ref[...] = out

    def group(at, number):
        done = []
        for h in range(GROUP):
            lanes = lanes_of(at, h)
            head = number * GROUP + h
            rate = column(rate_ref, head)
            coef = column(coef_ref, head)
            state = read_head(s_ref, at, h, 0)
            later = read_head(s_ref, at, h, 8)
            inflow = stacked(coef * jnp.exp(-rate * (spot + 1.0)), (0, 0, 1))
            outflow = stacked(coef * jnp.exp(-rate * (float(rows) - spot)), (0, 0, 1))
            conv = conv_ref[:, lanes] + mm_tn(inflow, stacked(state))
            done.append((mixed_ref, lanes, (q_ref[:, lanes].astype(F32) * conv).astype(BF16)))
            done.append((gq_ref, lanes, (c_ref[:, lanes].astype(F32) * conv).astype(BF16)))
            grad = grad_ref[:, lanes] + mm_tn(outflow, stacked(later))
            done.append((gk_ref, lanes, (grad * v_ref[:, lanes].astype(F32)).astype(BF16)))
            done.append((gv_ref, lanes, (grad * k_ref[:, lanes].astype(F32)).astype(BF16)))
        for ref, lanes, value in done:
            ref[:, lanes] = value

    each_batch(BATCH["outputs"], lambda groups: [group(*g) for g in groups])


def on_device(query, key_in, value, cotangent, decay_rate, residue):
    blocks = lax.axis_size("ctx") * lax.axis_size("head")
    place = lax.axis_index("ctx") * lax.axis_size("head") + lax.axis_index("head")
    rows, width = query.shape
    chunks = rows // CHUNK
    steps = GROUPS // PACK
    scale = 1.0 / math.sqrt(float(rows * blocks * WIDTH))
    rates = decay_rate.T
    norms = jnp.sqrt(-jnp.expm1(-2.0 * rates))
    coefs = residue.T * norms

    wide = pl.BlockSpec((rows, PACK * GROUP * WIDTH), lambda g: (0, g))
    small = pl.BlockSpec((POLES, HEADS), lambda g: (0, 0))
    fixed = pl.BlockSpec((8, WIDTH), lambda g: (0, 0))
    tile = pl.BlockSpec((PACK * OWNERS, 16, WIDTH), lambda g: (g, 0, 0))
    part = pl.BlockSpec((PACK * GROUP, 2, chunks * POLES, WIDTH), lambda g: (g, 0, 0, 0))
    wide_bytes = 2 * rows * width
    out16 = jax.ShapeDtypeStruct((rows, width), BF16)
    out32 = jax.ShapeDtypeStruct((rows, width), F32)
    line = jax.ShapeDtypeStruct((8, WIDTH), F32)
    tiles = jax.ShapeDtypeStruct((GROUPS * OWNERS, 16, WIDTH), F32)
    part_out = jax.ShapeDtypeStruct((HEADS, 2, chunks * POLES, WIDTH), F32)

    def call(kernel, name, grid, in_specs, out_specs, out_shape, passes, limit=None, scratch=(), **fixed_args):
        return pl.pallas_call(
            functools.partial(kernel, **fixed_args),
            grid=grid,
            in_specs=in_specs,
            out_specs=out_specs,
            out_shape=out_shape,
            scratch_shapes=scratch,
            cost_estimate=pl.CostEstimate(
                flops=10**9 * passes, bytes_accessed=passes * wide_bytes, transcendentals=0
            ),
            compiler_params=pltpu.CompilerParams(vmem_limit_bytes=limit),
            name=name,
        )

    gates = (query, key_in, value, cotangent)
    states = call(states_kernel, "states", (steps,), [small, wide, wide, wide, wide], tile, tiles, 4)(rates, *gates)
    gathered = lax.all_to_all(states, ("ctx", "head"), split_axis=0, concat_axis=0, tiled=True)

    near, parts, *products = call(
        near_kernel,
        "near",
        (steps,),
        [small, small, wide, wide, wide, wide],
        [fixed, part, wide, wide, wide, wide],
        [line, part_out, out16, out16, out16, out16],
        9,
        scale=scale,
    )(rates, norms, *gates)

    conv, grad = call(
        local_kernel,
        "local",
        (steps,),
        [small, small, part, wide, wide, wide, wide],
        [wide, wide],
        [out32, out32],
        9,
    )(rates, coefs, parts, *products)

    whole = pl.BlockSpec(memory_space=pltpu.VMEM)
    scanned = call(
        scan_kernel,
        "scan",
        (),
        [pl.BlockSpec(memory_space=pltpu.SMEM), whole, whole, whole, whole],
        whole,
        tiles,
        1,
        limit=VMEM_LIMIT,
        block_rows=rows,
        scale=scale,
    )(place.reshape(1), rates, norms, near, gathered)
    entering = lax.all_to_all(scanned, ("ctx", "head"), split_axis=0, concat_axis=0, tiled=True)

    *outs, res = call(
        output_kernel,
        "outputs",
        (steps,),
        [small, small, tile, wide, wide, wide, wide, wide, wide],
        [wide, wide, wide, wide, pl.BlockSpec((POLES, HEADS // 2), lambda g: (0, 0))],
        [out16, out16, out16, out16, jax.ShapeDtypeStruct((POLES, HEADS // 2), F32)],
        12,
        scratch=[pltpu.VMEM((8, WIDTH), F32)],
    )(rates, coefs, entering, *gates, conv, grad)
    return (*outs, res.T)


def solution(mesh):
    wide = P(("ctx", "head"), None)
    return jax.shard_map(
        on_device,
        mesh=mesh,
        in_specs=(wide, wide, wide, wide, P(), P()),
        out_specs=(wide, wide, wide, wide, P("head", None)),
        check_vma=False,
    )
```

time: 1050 us -> 78.8 us (0.08); the launches traced: 1030 us -> 78.3 us
  blocking collectives: 678 us -> 0 us
  local copies, waits for them, and re-layouts: 132 us -> 1.66 us
  matrix products: 116 us -> 0 us
  other arithmetic: 78.4 us -> 0.62 us
  Pallas kernels: 0 us -> 45.8 us
  between operations: 14.5 us -> 0.69 us
  waiting for transfers between devices: 0.04 us -> 13.7 us
    psum x1 -> x0, blocking collectives: 399 us -> none  [on_device(): residue_grad = lax.psum(results[4], 'ctx')]
    all_gather x1 -> x0, blocking collectives: 155 us -> none  [entering_2(): gathered = jax.tree.map(lambda a: lax.all_gather(a, axis), part)]
    all_to_all x6 -> x0, blocking collectives: 123 us -> none  [the longest x1 62.1 us: on_device(): lax.all_to_all(results[2], 'head', split_axis=0, concat_axis=1, tiled=True)]
    dot_general x9 -> x0, matrix products: 116 us -> none  [the longest x1 23.5 us: modal_layer(): jnp.einsum('hij,bjhc->bihc', toeplitz, product, precision=HIGHEST)]
    add x64 -> x0, other arithmetic: 66.9 us -> none  [the longest x63 66.1 us: combine_states(): later_part[0][..., None] * earlier[1] + later_part[1]]
    convert_element_type x12 -> x0, local copies, waits for them, and re-layouts: 46.4 us -> none  [the longest x4 24.3 us: blocked(): source.reshape(block_count, block_rows, head_count, head_size)]
    pallas_call x0 -> x5, Pallas kernels: none -> 45.8 us  [the longest x1 12.7 us: on_device(): call(near_kernel, 'near', (steps,), [small, small, wide, wide, wide, wide...]
    mul x63 -> x0, local copies, waits for them, and re-layouts: 44.9 us -> none  [combine_states(): later_part[0][..., None] * earlier[1] + later_part[1]]
  transfers between devices with their start and end apart: 4 -> 2, of which waited for: 0 -> 2; matrix products, arithmetic and copies ran while one was open for 17% -> 1% of each run, Pallas kernels for 0% -> 31%
where the time goes in v2:
time: 78.8 us; the launch traced here: 78.3 us
  Pallas kernels  45.8 us (58%)
  starting transfers between devices  15.9 us (20%)
  waiting for transfers between devices  13.7 us (17%)
  local copies, waits for them, and re-layouts  1.66 us (2%)
    pallas_call x1, Pallas kernels, on_device(): call(near_kernel, 'near', (steps,), [small, small, wide, wide, wide, wide...  12.7 us
    pallas_call x1, Pallas kernels, on_device(): call(output_kernel, 'outputs', (steps,), [small, small, tile, wide, wide,...  12.4 us
    pallas_call x1, Pallas kernels, on_device(): call(local_kernel, 'local', (steps,), [small, small, part, wide, wide, wi...  11.6 us
    all_to_all x1, starting transfers between devices, on_device(): lax.all_to_all(states, ('ctx', 'head'), split_axis=0, concat_axis=0, tile...  11.5 us
    all_to_all x1, waiting for transfers between devices, on_device(): lax.all_to_all(scanned, ('ctx', 'head'), split_axis=0, concat_axis=0, til...  7.77 us
    pallas_call x1, Pallas kernels, on_device(): call(states_kernel, 'states', (steps,), [small, wide, wide, wide, wide],...  7.28 us
    all_to_all x1, waiting for transfers between devices, on_device(): lax.all_to_all(states, ('ctx', 'head'), split_axis=0, concat_axis=0, tile...  5.9 us
    all_to_all x1, starting transfers between devices, on_device(): lax.all_to_all(scanned, ('ctx', 'head'), split_axis=0, concat_axis=0, til...  4.43 us
  transfers between devices with their start and end apart: 2, of which 2 were waited for; matrix products, arithmetic and copies ran while one was open for 1% of the time, Pallas kernels for 31%

profile of v2, /device:TPU:1, one launch (start us, length us, event | category | flops | bytes accessed | tf_op | source)
XLA Modules:
  0.0 78.3 jit_solution(11459325865621066229)
XLA Ops:
  0.6 0.0 copy-start
  0.6 0.0 copy-start.5
  0.7 7.3 %states.1 = f32[128,16,128]{2,1,0:T(8,128)} custom-call(f32[16,48]{1,0:T(8,128)} %bitcast.8, bf16[192,6144]{1,0:T(8,128)(2,1)} %q_ref.5, bf16[192,6144]{1,0:T(8,128)(2,1)} %k_ref.5, bf16[192,6144]{1,0:T(8,128)(2,1)} %v_ref.5, bf16[192,6144]{1,0:T(8,128)(2,1)} %c_ref.5), custom_call_target="tpu_custom_call" | custom-call | flops 4000000000 | bytes 9437184 | tf_op jit(solution)/shard_map/states/pallas_call | solution.py:383
  7.9 11.5 %all-to-all-start = ((f32[128,16,128]{2,1,0:T(8,128)}), f32[128,16,128]{2,1,0:T(8,128)S(1)}, u32[]{:S(2)}, u32[]{:S(2)}) async-start(f32[128,16,128]{2,1,0:T(8,128)} %states.1), calls=%async_computation | async-start | bytes 2097152 | tf_op jit(solution)/shard_map/all_to_all | solution.py:384
  19.4 0.0 copy-done
  19.4 0.0 copy-done.5
  19.4 0.6 negate_sqrt_fusion
  20.1 0.0 copy-start.1
  20.1 0.0 copy-start.2
  20.1 12.7 %near.1 = (f32[8,128]{1,0:T(8,128)}, f32[48,2,48,128]{3,2,1,0:T(8,128)}, bf16[192,6144]{1,0:T(8,128)(2,1)}, bf16[192,6144]{1,0:T(8,128)(2,1)}, bf16[192,6144]{1,0:T(8,128)(2,1)}, /*index=5*/bf16[192,6144]{1,0:T(8,128)(2,1)}) custom-call(f32[16,48]{1,0:T(8,128)} %bitcast.9, f32[16,48]{1,0:T(8,128)} %get-tuple-element.31.norm_ref, bf16[192,6144]{1,0:T(8,128)(2,1)} %q_ref.5, ...), custom_call_target="tpu_custom_call" | custom-call | flops 8999999488 | bytes 21233664 | tf_op jit(solution)/shard_map/near/pallas_call | solution.py:386
  32.8 5.9 %all-to-all-done.x_ref = f32[128,16,128]{2,1,0:T(8,128)S(1)} async-done(((f32[128,16,128]{2,1,0:T(8,128)}), f32[128,16,128]{2,1,0:T(8,128)S(1)}, u32[]{:S(2)}, u32[]{:S(2)}) %all-to-all-start) | async-done | bytes 1048608 | tf_op jit(solution)/shard_map/all_to_all | solution.py:384
  38.6 0.0 copy-done.1
  38.7 0.0 copy-done.2
  38.7 0.0 copy-start.3
  38.7 0.7 copy-done.3
  39.3 1.9 %scan.1 = f32[128,16,128]{2,1,0:T(8,128)} custom-call(s32[1]{0:T(128)} %bitcast.2.place_ref, f32[16,48]{1,0:T(8,128)S(1)} %bitcast.12, f32[16,48]{1,0:T(8,128)S(1)} %copy-done.2, f32[8,128]{1,0:T(8,128)S(1)} %copy-done.3, f32[128,16,128]{2,1,0:T(8,128)S(1)} %all-to-all-done.x_ref), custom_call_target="tpu_custom_call" | custom-call | flops 1000000000 | bytes 2359296 | tf_op jit(solution)/shard_map/scan/pallas_call | solution.py:408
  41.2 4.4 %all-to-all-start.1 = ((f32[128,16,128]{2,1,0:T(8,128)}), f32[128,16,128]{2,1,0:T(8,128)S(1)}, u32[]{:S(2)}, u32[]{:S(2)}) async-start(f32[128,16,128]{2,1,0:T(8,128)} %scan.1), calls=%async_computation.1 | async-start | bytes 2097152 | tf_op jit(solution)/shard_map/all_to_all | solution.py:420
  45.7 11.6 %local.1 = (f32[192,6144]{1,0:T(8,128)}, f32[192,6144]{1,0:T(8,128)}) custom-call(f32[16,48]{1,0:T(8,128)} %bitcast.10, f32[16,48]{1,0:T(8,128)} %get-tuple-element.32.coef_ref, f32[48,2,48,128]{3,2,1,0:T(8,128)} %get-tuple-element.19.part_ref, bf16[192,6144]{1,0:T(8,128)(2,1)} %get-tuple-element.20.ph_ref, bf16[192,6144]{1,0:T(8,128)(2,1)} %get-tuple-element.21.pl_ref, ...), custom_call_target="tpu_custom_call" | custom-call | flops 8999999488 | bytes 21233664 | tf_op jit(solution)/shard_map/local/pallas_call | solution.py:397
  57.2 7.8 %all-to-all-done.1.s_ref = f32[128,16,128]{2,1,0:T(8,128)S(1)} async-done(((f32[128,16,128]{2,1,0:T(8,128)}), f32[128,16,128]{2,1,0:T(8,128)S(1)}, u32[]{:S(2)}, u32[]{:S(2)}) %all-to-all-start.1) | async-done | bytes 1048608 | tf_op jit(solution)/shard_map/all_to_all | solution.py:420
  65.0 0.0 copy-start.4
  65.0 1.0 %copy-done.4 = f32[128,16,128]{2,1,0:T(8,128)} copy-done((f32[128,16,128]{2,1,0:T(8,128)}, f32[128,16,128]{2,1,0:T(8,128)S(1)}, u32[]{:S(2)}) %copy-start.4) | copy-done | bytes 1048600
  66.0 12.4 %outputs.1 = (bf16[192,6144]{1,0:T(8,128)(2,1)}, bf16[192,6144]{1,0:T(8,128)(2,1)}, bf16[192,6144]{1,0:T(8,128)(2,1)}, bf16[192,6144]{1,0:T(8,128)(2,1)}, f32[16,24]{1,0:T(8,128)}) custom-call(f32[16,48]{1,0:T(8,128)} %bitcast.11, f32[16,48]{1,0:T(8,128)} %get-tuple-element.32.coef_ref, f32[128,16,128]{2,1,0:T(8,128)} %copy-done.4, bf16[192,6144]{1,0:T(8,128)(2,1)} %q_ref.5, ...), custom_call_target="tpu_custom_call" | custom-call | flops 12000000000 | bytes 28311552 | tf_op jit(solution)/shard_map/outputs/pallas_call | solution.py:422
Async XLA Ops:
  0.6 18.8 %copy-start = (f32[48,16]{0,1:T(8,128)S(1)}, f32[48,16]{0,1:T(8,128)}, u32[]{:S(2)}) copy-start(f32[48,16]{0,1:T(8,128)} %param.10) | copy-start | bytes 9220
  0.6 18.8 %copy-start.5 = (f32[48,16]{0,1:T(8,128)S(1)}, f32[48,16]{0,1:T(8,128)}, u32[]{:S(2)}) copy-start(f32[48,16]{0,1:T(8,128)} %param.11) | copy-start | bytes 9220
  7.9 30.7 %all-to-all-start = ((f32[128,16,128]{2,1,0:T(8,128)}), f32[128,16,128]{2,1,0:T(8,128)S(1)}, u32[]{:S(2)}, u32[]{:S(2)}) async-start(f32[128,16,128]{2,1,0:T(8,128)} %states.1), calls=%async_computation | async-start | bytes 2097152 | tf_op jit(solution)/shard_map/all_to_all | solution.py:384
  20.1 18.6 %copy-start.1 = (f32[48,16]{0,1:T(8,128)S(1)}, f32[48,16]{0,1:T(8,128)}, u32[]{:S(2)}) copy-start(f32[48,16]{0,1:T(8,128)} %param.10) | copy-start | bytes 9220
  20.1 18.6 %copy-start.2 = (f32[16,48]{1,0:T(8,128)S(1)}, f32[16,48]{1,0:T(8,128)}, u32[]{:S(2)}) copy-start(f32[16,48]{1,0:T(8,128)} %get-tuple-element.31.norm_ref) | copy-start | bytes 9220
  38.7 0.7 copy-start.3
  41.2 23.8 %all-to-all-start.1 = ((f32[128,16,128]{2,1,0:T(8,128)}), f32[128,16,128]{2,1,0:T(8,128)S(1)}, u32[]{:S(2)}, u32[]{:S(2)}) async-start(f32[128,16,128]{2,1,0:T(8,128)} %scan.1), calls=%async_computation.1 | async-start | bytes 2097152 | tf_op jit(solution)/shard_map/all_to_all | solution.py:420
  65.0 1.0 %copy-start.4 = (f32[128,16,128]{2,1,0:T(8,128)}, f32[128,16,128]{2,1,0:T(8,128)S(1)}, u32[]{:S(2)}) copy-start(f32[128,16,128]{2,1,0:T(8,128)S(1)} %all-to-all-done.1.s_ref) | copy-start | bytes 3145732

commit v3 on v2

--- a/solution.py
+++ b/solution.py
@@ -21,6 +21,9 @@
 F32 = jnp.float32
 BF16 = jnp.bfloat16
 VMEM_LIMIT = 12 * 2**20
+OUT_LIMIT = 51 * 2**20
+LOCAL_LIMIT = None
+OUT_PACK = 4
 
 
 def split(x):
@@ -62,12 +65,12 @@
     return pl.ds(pl.multiple_of((at * GROUP + h) * WIDTH, WIDTH), WIDTH)
 
 
-def each_batch(batch, body):
+def each_batch(batch, body, pack=PACK):
     def lap(n, _):
-        body([(n * batch + j, pl.program_id(0) * PACK + n * batch + j) for j in range(batch)])
+        body([(n * batch + j, pl.program_id(0) * pack + n * batch + j) for j in range(batch)])
         return 0
 
-    lax.fori_loop(0, PACK // batch, lap, 0)
+    lax.fori_loop(0, pack // batch, lap, 0)
 
 
 def sublane_of(owner, unit):
@@ -229,7 +232,9 @@
     each_batch(BATCH["local"], batch)
 
 
-def scan_kernel(place_ref, rate_ref, norm_ref, near_ref, x_ref, out_ref, *, block_rows, scale):
+def scan_kernel(place_ref, rate_ref, norm_ref, near_hbm, x_ref, out_ref, near_ref, arrived, *, block_rows, scale):
+    fetch = pltpu.make_async_copy(near_hbm, near_ref, arrived)
+    fetch.start()
     blocks = x_ref.shape[0]
     group = place_ref[0] // OWNERS
     owner = lax.rem(place_ref[0], OWNERS)
@@ -248,12 +253,16 @@
     rate = own(rate_ref)
     over = jnp.exp(-rate * float(block_rows))
 
-    def forward(e, carry):
-        state, far = carry
+    def both(e, carry):
+        state, adjoint, far = carry
+        back = blocks - 1 - e
         out_ref[e, :8, :] = state
-        return over * state + x_ref[e, :8, :], far + x_ref[e, 8:, :] * state
-
-    _, far = lax.fori_loop(0, blocks, forward, (zero, zero), unroll=8)
+        out_ref[back, 8:, :] = adjoint
+        far += x_ref[e, 8:, :] * state
+        return over * state + x_ref[e, :8, :], over * adjoint + x_ref[back, 8:, :], far
+
+    _, _, far = lax.fori_loop(0, blocks, both, (zero, zero, zero), unroll=8)
+    fetch.wait()
     far = jnp.sum(far * jnp.exp(-rate), axis=1, keepdims=True) * own(norm_ref) * scale
     total = near_ref[...]
     for u in range(UNITS):
@@ -271,15 +280,14 @@
             for k in range(2):
                 pads[k][side] = jnp.where(at, total[3 * k + line : 3 * k + line + 1], pads[k][side])
 
-    def backward(lap, state):
-        for k in (1, 0):
-            e = blocks - 2 - 2 * lap + k
+    def spare(lap, _):
+        for k in range(2):
+            e = 2 * lap + k
             out_ref[e, :8, :] = jnp.where(used, out_ref[e, :8, :], pads[k][0])
-            out_ref[e, 8:, :] = jnp.where(used, state, pads[k][1])
-            state = over * state + x_ref[e, 8:, :]
-        return state
-
-    lax.fori_loop(0, blocks // 2, backward, zero, unroll=4)
+            out_ref[e, 8:, :] = jnp.where(used, out_ref[e, 8:, :], pads[k][1])
+        return 0
+
+    lax.fori_loop(0, blocks // 2, spare, 0, unroll=8)
 
 
 def output_kernel(
@@ -296,12 +304,12 @@
         sums[...] = jnp.zeros_like(sums)
 
     res = sums[...]
-    for at in range(PACK):
+    for at in range(OUT_PACK):
         for u, first, line in ((6, 0, 0), (7, 0, 1), (6, 8, 2)):
             value = jnp.zeros((1, WIDTH), F32)
             for owner in range(OWNERS):
                 row = first + (owner - u) % 8
-                value += s_ref[at * OWNERS + owner, row : row + 1, :]
+                value += s_ref[(step * OUT_PACK + at) * OWNERS + owner, row : row + 1, :]
             res += jnp.where(sub == line, value, 0.0)
     sums[...] = res
 
@@ -318,27 +326,31 @@
             out += mm(high, pick) + mm(low, pick)
         res_ref[...] = out
 
-    def group(at, number):
-        done = []
-        for h in range(GROUP):
-            lanes = lanes_of(at, h)
-            head = number * GROUP + h
-            rate = column(rate_ref, head)
-            coef = column(coef_ref, head)
-            state = read_head(s_ref, at, h, 0)
-            later = read_head(s_ref, at, h, 8)
-            inflow = stacked(coef * jnp.exp(-rate * (spot + 1.0)), (0, 0, 1))
-            outflow = stacked(coef * jnp.exp(-rate * (float(rows) - spot)), (0, 0, 1))
-            conv = conv_ref[:, lanes] + mm_tn(inflow, stacked(state))
+    def batch(groups):
+        heads = [(number, h, lanes_of(at, h)) for at, number in groups for h in range(GROUP)]
+        tables, done = [], []
+        for number, h, _ in heads:
+            rate = column(rate_ref, number * GROUP + h)
+            coef = column(coef_ref, number * GROUP + h)
+            tables.append(
+                (
+                    stacked(coef * jnp.exp(-rate * (spot + 1.0)), (0, 0, 1)),
+                    stacked(read_head(s_ref, number, h, 0)),
+                    stacked(coef * jnp.exp(-rate * (float(rows) - spot)), (0, 0, 1)),
+                    stacked(read_head(s_ref, number, h, 8)),
+                )
+            )
+        for (inflow, state, outflow, later), (_, _, lanes) in zip(tables, heads):
+            conv = conv_ref[:, lanes] + mm_tn(inflow, state)
             done.append((mixed_ref, lanes, (q_ref[:, lanes].astype(F32) * conv).astype(BF16)))
             done.append((gq_ref, lanes, (c_ref[:, lanes].astype(F32) * conv).astype(BF16)))
-            grad = grad_ref[:, lanes] + mm_tn(outflow, stacked(later))
+            grad = grad_ref[:, lanes] + mm_tn(outflow, later)
             done.append((gk_ref, lanes, (grad * v_ref[:, lanes].astype(F32)).astype(BF16)))
             done.append((gv_ref, lanes, (grad * k_ref[:, lanes].astype(F32)).astype(BF16)))
         for ref, lanes, value in done:
             ref[:, lanes] = value
 
-    each_batch(BATCH["outputs"], lambda groups: [group(*g) for g in groups])
+    each_batch(BATCH["outputs"], batch, OUT_PACK)
 
 
 def on_device(query, key_in, value, cotangent, decay_rate, residue):
@@ -353,6 +365,7 @@
     coefs = residue.T * norms
 
     wide = pl.BlockSpec((rows, PACK * GROUP * WIDTH), lambda g: (0, g))
+    thin = pl.BlockSpec((rows, OUT_PACK * GROUP * WIDTH), lambda g: (0, g))
     small = pl.BlockSpec((POLES, HEADS), lambda g: (0, 0))
     fixed = pl.BlockSpec((8, WIDTH), lambda g: (0, 0))
     tile = pl.BlockSpec((PACK * OWNERS, 16, WIDTH), lambda g: (g, 0, 0))
@@ -402,6 +415,7 @@
         [wide, wide],
         [out32, out32],
         9,
+        limit=LOCAL_LIMIT,
     )(rates, coefs, parts, *products)
 
     whole = pl.BlockSpec(memory_space=pltpu.VMEM)
@@ -409,11 +423,12 @@
         scan_kernel,
         "scan",
         (),
-        [pl.BlockSpec(memory_space=pltpu.SMEM), whole, whole, whole, whole],
+        [pl.BlockSpec(memory_space=pltpu.SMEM), whole, whole, pl.BlockSpec(memory_space=pltpu.HBM), whole],
         whole,
         tiles,
         1,
         limit=VMEM_LIMIT,
+        scratch=[pltpu.VMEM((8, WIDTH), F32), pltpu.SemaphoreType.DMA],
         block_rows=rows,
         scale=scale,
     )(place.reshape(1), rates, norms, near, gathered)
@@ -422,11 +437,12 @@
     *outs, res = call(
         output_kernel,
         "outputs",
-        (steps,),
-        [small, small, tile, wide, wide, wide, wide, wide, wide],
-        [wide, wide, wide, wide, pl.BlockSpec((POLES, HEADS // 2), lambda g: (0, 0))],
+        (GROUPS // OUT_PACK,),
+        [small, small, whole, thin, thin, thin, thin, thin, thin],
+        [thin, thin, thin, thin, pl.BlockSpec((POLES, HEADS // 2), lambda g: (0, 0))],
         [out16, out16, out16, out16, jax.ShapeDtypeStruct((POLES, HEADS // 2), F32)],
         12,
+        limit=OUT_LIMIT,
         scratch=[pltpu.VMEM((8, WIDTH), F32)],
     )(rates, coefs, entering, *gates, conv, grad)
     return (*outs, res.T)

time: 78.8 us -> 76.9 us (0.976)
  local copies, waits for them, and re-layouts: 1.66 us -> 0.7 us
    unnamed x12 -> x14, local copies, waits for them, and re-layouts: 1.66 us -> 0.7 us
  transfers between devices with their start and end apart: 2 -> 2, of which waited for: 2 -> 2; matrix products, arithmetic and copies ran while one was open for 1% -> 1% of each run, Pallas kernels for 31% -> 32%
where the time goes in v3:
time: 76.9 us; the launch traced here: 76.4 us
  Pallas kernels  45.2 us (59%)
  starting transfers between devices  15.9 us (21%)
  waiting for transfers between devices  13.3 us (17%)
    pallas_call x1, Pallas kernels, on_device(): call(near_kernel, 'near', (steps,), [small, small, wide, wide, wide, wide...  12.7 us
    pallas_call x1, Pallas kernels, on_device(): call(local_kernel, 'local', (steps,), [small, small, part, wide, wide, wi...  12 us
    pallas_call x1, Pallas kernels, on_device(): call(output_kernel, 'outputs', (GROUPS // OUT_PACK,), [small, small, whol...  11.7 us
    all_to_all x1, starting transfers between devices, on_device(): lax.all_to_all(states, ('ctx', 'head'), split_axis=0, concat_axis=0, tile...  11.5 us
    all_to_all x1, waiting for transfers between devices, on_device(): lax.all_to_all(scanned, ('ctx', 'head'), split_axis=0, concat_axis=0, til...  7.36 us
    pallas_call x1, Pallas kernels, on_device(): call(states_kernel, 'states', (steps,), [small, wide, wide, wide, wide],...  7.29 us
    all_to_all x1, waiting for transfers between devices, on_device(): lax.all_to_all(states, ('ctx', 'head'), split_axis=0, concat_axis=0, tile...  5.92 us
    all_to_all x1, starting transfers between devices, on_device(): lax.all_to_all(scanned, ('ctx', 'head'), split_axis=0, concat_axis=0, til...  4.43 us
  transfers between devices with their start and end apart: 2, of which 2 were waited for; matrix products, arithmetic and copies ran while one was open for 1% of the time, Pallas kernels for 32%

profile of v3, /device:TPU:1, one launch (start us, length us, event | category | flops | bytes accessed | tf_op | source)
XLA Modules:
  0.0 76.4 jit_solution(3559691124638308492)
XLA Ops:
  0.6 0.0 copy-start
  0.6 0.0 copy-start.6
  0.7 7.3 %states.1 = f32[128,16,128]{2,1,0:T(8,128)} custom-call(f32[16,48]{1,0:T(8,128)} %bitcast.8, bf16[192,6144]{1,0:T(8,128)(2,1)} %q_ref.5, bf16[192,6144]{1,0:T(8,128)(2,1)} %k_ref.5, bf16[192,6144]{1,0:T(8,128)(2,1)} %v_ref.5, bf16[192,6144]{1,0:T(8,128)(2,1)} %c_ref.5), custom_call_target="tpu_custom_call" | custom-call | flops 4000000000 | bytes 9437184 | tf_op jit(solution)/shard_map/states/pallas_call | solution.py:396
  7.9 11.5 %all-to-all-start = ((f32[128,16,128]{2,1,0:T(8,128)}), f32[128,16,128]{2,1,0:T(8,128)S(1)}, u32[]{:S(2)}, u32[]{:S(2)}) async-start(f32[128,16,128]{2,1,0:T(8,128)} %states.1), calls=%async_computation | async-start | bytes 2097152 | tf_op jit(solution)/shard_map/all_to_all | solution.py:397
  19.4 0.0 copy-done
  19.4 0.0 copy-done.6
  19.5 0.6 negate_sqrt_fusion
  20.1 0.0 copy-start.1
  20.1 0.0 copy-start.4
  20.1 12.7 %near.1 = (f32[8,128]{1,0:T(8,128)}, f32[48,2,48,128]{3,2,1,0:T(8,128)}, bf16[192,6144]{1,0:T(8,128)(2,1)}, bf16[192,6144]{1,0:T(8,128)(2,1)}, bf16[192,6144]{1,0:T(8,128)(2,1)}, /*index=5*/bf16[192,6144]{1,0:T(8,128)(2,1)}) custom-call(f32[16,48]{1,0:T(8,128)} %bitcast.9, f32[16,48]{1,0:T(8,128)} %get-tuple-element.31.norm_ref, bf16[192,6144]{1,0:T(8,128)(2,1)} %q_ref.5, ...), custom_call_target="tpu_custom_call" | custom-call | flops 8999999488 | bytes 21233664 | tf_op jit(solution)/shard_map/near/pallas_call | solution.py:399
  32.7 5.9 %all-to-all-done.x_ref = f32[128,16,128]{2,1,0:T(8,128)S(1)} async-done(((f32[128,16,128]{2,1,0:T(8,128)}), f32[128,16,128]{2,1,0:T(8,128)S(1)}, u32[]{:S(2)}, u32[]{:S(2)}) %all-to-all-start) | async-done | bytes 1048608 | tf_op jit(solution)/shard_map/all_to_all | solution.py:397
  38.7 0.0 copy-done.1
  38.7 0.0 copy-done.4
  38.7 0.0 copy-start.5
  38.7 0.7 copy-done.5
  39.3 1.6 %scan.1 = f32[128,16,128]{2,1,0:T(8,128)} custom-call(s32[1]{0:T(128)} %bitcast.2.place_ref, f32[16,48]{1,0:T(8,128)S(1)} %bitcast.11, f32[16,48]{1,0:T(8,128)S(1)} %copy-done.4, f32[8,128]{1,0:T(8,128)S(1)} %copy-done.5, f32[128,16,128]{2,1,0:T(8,128)S(1)} %all-to-all-done.x_ref), custom_call_target="tpu_custom_call" | custom-call | flops 1000000000 | bytes 2359296 | tf_op jit(solution)/shard_map/scan/pallas_call | solution.py:422
  40.9 4.4 %all-to-all-start.1 = ((f32[128,16,128]{2,1,0:T(8,128)}), f32[128,16,128]{2,1,0:T(8,128)S(1)}, u32[]{:S(2)}, u32[]{:S(2)}) async-start(f32[128,16,128]{2,1,0:T(8,128)} %scan.1), calls=%async_computation.1 | async-start | bytes 2097152 | tf_op jit(solution)/shard_map/all_to_all | solution.py:435
  45.4 0.0 copy-start.2
  45.4 0.0 copy-start.3
  45.4 12.0 %local.1 = (f32[192,6144]{1,0:T(8,128)}, f32[192,6144]{1,0:T(8,128)}) custom-call(f32[16,48]{1,0:T(8,128)} %bitcast.10, f32[16,48]{1,0:T(8,128)} %get-tuple-element.32.coef_ref, f32[48,2,48,128]{3,2,1,0:T(8,128)} %get-tuple-element.19.part_ref, bf16[192,6144]{1,0:T(8,128)(2,1)} %get-tuple-element.20.ph_ref, bf16[192,6144]{1,0:T(8,128)(2,1)} %get-tuple-element.21.pl_ref, ...), custom_call_target="tpu_custom_call" | custom-call | flops 8999999488 | bytes 21233664 | tf_op jit(solution)/shard_map/local/pallas_call | solution.py:410
  57.4 7.4 %all-to-all-done.1.s_ref = f32[128,16,128]{2,1,0:T(8,128)S(1)} async-done(((f32[128,16,128]{2,1,0:T(8,128)}), f32[128,16,128]{2,1,0:T(8,128)S(1)}, u32[]{:S(2)}, u32[]{:S(2)}) %all-to-all-start.1) | async-done | bytes 1048608 | tf_op jit(solution)/shard_map/all_to_all | solution.py:435
  64.7 0.0 copy-done.2
  64.7 0.0 copy-done.3
  64.7 11.7 %outputs.1 = (bf16[192,6144]{1,0:T(8,128)(2,1)}, bf16[192,6144]{1,0:T(8,128)(2,1)}, bf16[192,6144]{1,0:T(8,128)(2,1)}, bf16[192,6144]{1,0:T(8,128)(2,1)}, f32[16,24]{1,0:T(8,128)}) custom-call(f32[16,48]{1,0:T(8,128)S(1)} %bitcast.12, f32[16,48]{1,0:T(8,128)S(1)} %copy-done.3, f32[128,16,128]{2,1,0:T(8,128)S(1)} %all-to-all-done.1.s_ref, ...), custom_call_target="tpu_custom_call" | custom-call | flops 12000000000 | bytes 28311552 | tf_op jit(solution)/shard_map/outputs/pallas_call | solution.py:437
Async XLA Ops:
  0.6 18.8 %copy-start = (f32[48,16]{0,1:T(8,128)S(1)}, f32[48,16]{0,1:T(8,128)}, u32[]{:S(2)}) copy-start(f32[48,16]{0,1:T(8,128)} %param.10) | copy-start | bytes 9220
  0.6 18.8 %copy-start.6 = (f32[48,16]{0,1:T(8,128)S(1)}, f32[48,16]{0,1:T(8,128)}, u32[]{:S(2)}) copy-start(f32[48,16]{0,1:T(8,128)} %param.11) | copy-start | bytes 9220
  7.9 30.7 %all-to-all-start = ((f32[128,16,128]{2,1,0:T(8,128)}), f32[128,16,128]{2,1,0:T(8,128)S(1)}, u32[]{:S(2)}, u32[]{:S(2)}) async-start(f32[128,16,128]{2,1,0:T(8,128)} %states.1), calls=%async_computation | async-start | bytes 2097152 | tf_op jit(solution)/shard_map/all_to_all | solution.py:397
  20.1 18.6 %copy-start.1 = (f32[48,16]{0,1:T(8,128)S(1)}, f32[48,16]{0,1:T(8,128)}, u32[]{:S(2)}) copy-start(f32[48,16]{0,1:T(8,128)} %param.10) | copy-start | bytes 9220
  20.1 18.6 %copy-start.4 = (f32[16,48]{1,0:T(8,128)S(1)}, f32[16,48]{1,0:T(8,128)}, u32[]{:S(2)}) copy-start(f32[16,48]{1,0:T(8,128)} %get-tuple-element.31.norm_ref) | copy-start | bytes 9220
  38.7 0.7 copy-start.5
  40.9 23.8 %all-to-all-start.1 = ((f32[128,16,128]{2,1,0:T(8,128)}), f32[128,16,128]{2,1,0:T(8,128)S(1)}, u32[]{:S(2)}, u32[]{:S(2)}) async-start(f32[128,16,128]{2,1,0:T(8,128)} %scan.1), calls=%async_computation.1 | async-start | bytes 2097152 | tf_op jit(solution)/shard_map/all_to_all | solution.py:435
  45.4 19.3 %copy-start.2 = (f32[48,16]{0,1:T(8,128)S(1)}, f32[48,16]{0,1:T(8,128)}, u32[]{:S(2)}) copy-start(f32[48,16]{0,1:T(8,128)} %param.10) | copy-start | bytes 9220
  45.4 19.3 %copy-start.3 = (f32[16,48]{1,0:T(8,128)S(1)}, f32[16,48]{1,0:T(8,128)}, u32[]{:S(2)}) copy-start(f32[16,48]{1,0:T(8,128)} %get-tuple-element.32.coef_ref) | copy-start | bytes 9220

commit v4 on v3

--- a/solution.py
+++ b/solution.py
@@ -22,6 +22,7 @@
 BF16 = jnp.bfloat16
 VMEM_LIMIT = 12 * 2**20
 OUT_LIMIT = 51 * 2**20
+NEAR_LIMIT = 51 * 2**20
 LOCAL_LIMIT = None
 OUT_PACK = 4
 
@@ -404,6 +405,7 @@
         [fixed, part, wide, wide, wide, wide],
         [line, part_out, out16, out16, out16, out16],
         9,
+        limit=NEAR_LIMIT,
         scale=scale,
     )(rates, norms, *gates)
 

time: 76.9 us -> 76.2 us (level)
  Pallas kernels: 45.2 us -> 44.1 us
    pallas_call x1, Pallas kernels: 12.7 us -> 11.6 us  [on_device(): call(near_kernel, 'near', (steps,), [small, small, wide, wide, wide, wide...]
  transfers between devices with their start and end apart: 2 -> 2, of which waited for: 2 -> 2; matrix products, arithmetic and copies ran while one was open for 1% -> 1% of each run, Pallas kernels for 32% -> 31%
where the time goes in v4:
time: 76.2 us; the launch traced here: 75.7 us
  Pallas kernels  44.1 us (58%)
  starting transfers between devices  15.9 us (21%)
  waiting for transfers between devices  12.9 us (17%)
  local copies, waits for them, and re-layouts  1.41 us (2%)
    pallas_call x1, Pallas kernels, on_device(): call(local_kernel, 'local', (steps,), [small, small, part, wide, wide, wi...  11.9 us
    pallas_call x1, Pallas kernels, on_device(): call(output_kernel, 'outputs', (GROUPS // OUT_PACK,), [small, small, whol...  11.7 us
    pallas_call x1, Pallas kernels, on_device(): call(near_kernel, 'near', (steps,), [small, small, wide, wide, wide, wide...  11.6 us
    all_to_all x1, starting transfers between devices, on_device(): lax.all_to_all(states, ('ctx', 'head'), split_axis=0, concat_axis=0, tile...  11.5 us
    all_to_all x1, waiting for transfers between devices, on_device(): lax.all_to_all(scanned, ('ctx', 'head'), split_axis=0, concat_axis=0, til...  7.39 us
    pallas_call x1, Pallas kernels, on_device(): call(states_kernel, 'states', (steps,), [small, wide, wide, wide, wide],...  7.28 us
    all_to_all x1, waiting for transfers between devices, on_device(): lax.all_to_all(states, ('ctx', 'head'), split_axis=0, concat_axis=0, tile...  5.54 us
    all_to_all x1, starting transfers between devices, on_device(): lax.all_to_all(scanned, ('ctx', 'head'), split_axis=0, concat_axis=0, til...  4.43 us
  transfers between devices with their start and end apart: 2, of which 2 were waited for; matrix products, arithmetic and copies ran while one was open for 1% of the time, Pallas kernels for 31%

profile of v4, /device:TPU:1, one launch (start us, length us, event | category | flops | bytes accessed | tf_op | source)
XLA Modules:
  0.0 75.7 jit_solution(13115316787676439415)
XLA Ops:
  0.6 0.0 copy-start
  0.6 0.0 copy-start.4
  0.7 7.3 %states.1 = f32[128,16,128]{2,1,0:T(8,128)} custom-call(f32[16,48]{1,0:T(8,128)} %bitcast.8, bf16[192,6144]{1,0:T(8,128)(2,1)} %q_ref.5, bf16[192,6144]{1,0:T(8,128)(2,1)} %k_ref.5, bf16[192,6144]{1,0:T(8,128)(2,1)} %v_ref.5, bf16[192,6144]{1,0:T(8,128)(2,1)} %c_ref.5), custom_call_target="tpu_custom_call" | custom-call | flops 4000000000 | bytes 9437184 | tf_op jit(solution)/shard_map/states/pallas_call | solution.py:397
  7.9 11.5 %all-to-all-start = ((f32[128,16,128]{2,1,0:T(8,128)}), f32[128,16,128]{2,1,0:T(8,128)S(1)}, u32[]{:S(2)}, u32[]{:S(2)}) async-start(f32[128,16,128]{2,1,0:T(8,128)} %states.1), calls=%async_computation | async-start | bytes 2097152 | tf_op jit(solution)/shard_map/all_to_all | solution.py:398
  19.4 0.0 copy-done
  19.4 0.0 copy-done.4
  19.5 0.6 negate_sqrt_fusion
  20.1 11.6 %near.1 = (f32[8,128]{1,0:T(8,128)S(1)}, f32[48,2,48,128]{3,2,1,0:T(8,128)S(1)}, bf16[192,6144]{1,0:T(8,128)(2,1)}, bf16[192,6144]{1,0:T(8,128)(2,1)}, bf16[192,...) custom-call(f32[16,48]{1,0:T(8,128)S(1)} %bitcast.10, f32[16,48]{1,0:T(8,128)S(1)} %get-tuple-element.31.norm_ref, ...), custom_call_target="tpu_custom_call" | custom-call | flops 8999999488 | bytes 21233664 | tf_op jit(solution)/shard_map/near/pallas_call | solution.py:400
  31.7 0.0 copy-start.3
  31.7 1.4 %copy-done.3 = f32[48,2,48,128]{3,2,1,0:T(8,128)} copy-done((f32[48,2,48,128]{3,2,1,0:T(8,128)}, f32[48,2,48,128]{3,2,1,0:T(8,128)S(1)}, u32[]{:S(2)}) %copy-start.3) | copy-done | bytes 2359320
  33.1 5.5 %all-to-all-done.x_ref = f32[128,16,128]{2,1,0:T(8,128)S(1)} async-done(((f32[128,16,128]{2,1,0:T(8,128)}), f32[128,16,128]{2,1,0:T(8,128)S(1)}, u32[]{:S(2)}, u32[]{:S(2)}) %all-to-all-start) | async-done | bytes 1048608 | tf_op jit(solution)/shard_map/all_to_all | solution.py:398
  38.7 1.6 %scan.1 = f32[128,16,128]{2,1,0:T(8,128)} custom-call(s32[1]{0:T(128)} %bitcast.2.place_ref, f32[16,48]{1,0:T(8,128)S(1)} %bitcast.11, f32[16,48]{1,0:T(8,128)S(1)} %get-tuple-element.31.norm_ref, f32[8,128]{1,0:T(8,128)S(1)} %get-tuple-element.18.near_hbm, f32[128,16,128]{2,1,0:T(8,128)S(1)} %all-to-all-done.x_ref), custom_call_target="tpu_custom_call" | custom-call | flops 1000000000 | bytes 2359296 | tf_op jit(solution)/shard_map/scan/pallas_call | solution.py:424
  40.2 4.4 %all-to-all-start.1 = ((f32[128,16,128]{2,1,0:T(8,128)}), f32[128,16,128]{2,1,0:T(8,128)S(1)}, u32[]{:S(2)}, u32[]{:S(2)}) async-start(f32[128,16,128]{2,1,0:T(8,128)} %scan.1), calls=%async_computation.1 | async-start | bytes 2097152 | tf_op jit(solution)/shard_map/all_to_all | solution.py:437
  44.7 0.0 copy-start.1
  44.7 0.0 copy-start.2
  44.7 11.9 %local.1 = (f32[192,6144]{1,0:T(8,128)}, f32[192,6144]{1,0:T(8,128)}) custom-call(f32[16,48]{1,0:T(8,128)} %bitcast.9, f32[16,48]{1,0:T(8,128)} %get-tuple-element.32.coef_ref, f32[48,2,48,128]{3,2,1,0:T(8,128)} %copy-done.3, bf16[192,6144]{1,0:T(8,128)(2,1)} %get-tuple-element.20.ph_ref, bf16[192,6144]{1,0:T(8,128)(2,1)} %get-tuple-element.21.pl_ref, ...), custom_call_target="tpu_custom_call" | custom-call | flops 8999999488 | bytes 21233664 | tf_op jit(solution)/shard_map/local/pallas_call | solution.py:412
  56.6 7.4 %all-to-all-done.1.s_ref = f32[128,16,128]{2,1,0:T(8,128)S(1)} async-done(((f32[128,16,128]{2,1,0:T(8,128)}), f32[128,16,128]{2,1,0:T(8,128)S(1)}, u32[]{:S(2)}, u32[]{:S(2)}) %all-to-all-start.1) | async-done | bytes 1048608 | tf_op jit(solution)/shard_map/all_to_all | solution.py:437
  64.0 0.0 copy-done.1
  64.0 0.0 copy-done.2
  64.0 11.7 %outputs.1 = (bf16[192,6144]{1,0:T(8,128)(2,1)}, bf16[192,6144]{1,0:T(8,128)(2,1)}, bf16[192,6144]{1,0:T(8,128)(2,1)}, bf16[192,6144]{1,0:T(8,128)(2,1)}, f32[16,24]{1,0:T(8,128)}) custom-call(f32[16,48]{1,0:T(8,128)S(1)} %bitcast.12, f32[16,48]{1,0:T(8,128)S(1)} %copy-done.2, f32[128,16,128]{2,1,0:T(8,128)S(1)} %all-to-all-done.1.s_ref, ...), custom_call_target="tpu_custom_call" | custom-call | flops 12000000000 | bytes 28311552 | tf_op jit(solution)/shard_map/outputs/pallas_call | solution.py:439
Async XLA Ops:
  0.6 18.8 %copy-start = (f32[48,16]{0,1:T(8,128)S(1)}, f32[48,16]{0,1:T(8,128)}, u32[]{:S(2)}) copy-start(f32[48,16]{0,1:T(8,128)} %param.10) | copy-start | bytes 9220
  0.6 18.8 %copy-start.4 = (f32[48,16]{0,1:T(8,128)S(1)}, f32[48,16]{0,1:T(8,128)}, u32[]{:S(2)}) copy-start(f32[48,16]{0,1:T(8,128)} %param.11) | copy-start | bytes 9220
  7.9 30.7 %all-to-all-start = ((f32[128,16,128]{2,1,0:T(8,128)}), f32[128,16,128]{2,1,0:T(8,128)S(1)}, u32[]{:S(2)}, u32[]{:S(2)}) async-start(f32[128,16,128]{2,1,0:T(8,128)} %states.1), calls=%async_computation | async-start | bytes 2097152 | tf_op jit(solution)/shard_map/all_to_all | solution.py:398
  31.7 1.4 %copy-start.3 = (f32[48,2,48,128]{3,2,1,0:T(8,128)}, f32[48,2,48,128]{3,2,1,0:T(8,128)S(1)}, u32[]{:S(2)}) copy-start(f32[48,2,48,128]{3,2,1,0:T(8,128)S(1)} %get-tuple-element.19.part_ref) | copy-start | bytes 7077892
  40.2 23.8 %all-to-all-start.1 = ((f32[128,16,128]{2,1,0:T(8,128)}), f32[128,16,128]{2,1,0:T(8,128)S(1)}, u32[]{:S(2)}, u32[]{:S(2)}) async-start(f32[128,16,128]{2,1,0:T(8,128)} %scan.1), calls=%async_computation.1 | async-start | bytes 2097152 | tf_op jit(solution)/shard_map/all_to_all | solution.py:437
  44.7 19.3 %copy-start.1 = (f32[48,16]{0,1:T(8,128)S(1)}, f32[48,16]{0,1:T(8,128)}, u32[]{:S(2)}) copy-start(f32[48,16]{0,1:T(8,128)} %param.10) | copy-start | bytes 9220
  44.7 19.3 %copy-start.2 = (f32[16,48]{1,0:T(8,128)S(1)}, f32[16,48]{1,0:T(8,128)}, u32[]{:S(2)}) copy-start(f32[16,48]{1,0:T(8,128)} %get-tuple-element.32.coef_ref) | copy-start | bytes 9220
